TPU v7x, 256 devices: a whole 4x4x8 slice. The times are simulated.
256 devices in a mesh: mod: 64 (over x, z, core), tp: 4 (over y).
Axes of the slice: x: 4, y: 4, z: 8, core: 2. Of those that a mesh axis runs over, the one named last changes fastest.
Arguments:
- stream: bfloat16 [49152, 4096], P('mod'), as said below
- norm_gain: float32 [2, 4096], replicated, may hold values from 0.1 to 1.9
- qkv_weight: bfloat16 [2, 4096, 3, 2048], P(None, 'mod', None, 'tp'), may hold values from -0.09375 to 0.09375
- qk_gain: float32 [2, 2, 2048], P(None, None, 'tp'), may hold values from 0.6 to 2.5
- owner: int32 [32768], replicated, may hold values from 0 to 63, as said below
- doc_lengths: int32 [8, 4], replicated, may hold values from 1 to 2048, 4096 in all within a row
Outputs:
- context: bfloat16 [49152, 2048], P('mod', 'tp')
Inputs may be any that keep to these rules, and one draw needn't show every extreme that they name: `owner`: owners below 32 form the text section, the others the image section. In each aligned block of 256 tokens the text tokens form one contiguous run of 64 tokens; every text section device owns exactly 2 of them and every image section device exactly 6 of the image tokens of that block. Rows of stream that no token's slot names are never read.
All inputs are finite; a program needn't handle non-finite values.
Results may differ from a plain program's by a relative error of at most 0.011.
Values may be sent and summed in bfloat16 or wider, within the bound.
A program may use at most 128 MiB of HBM per device.

v0:
```python
import math

import jax
import jax.numpy as jnp
from jax import lax
from jax.sharding import PartitionSpec as P

HD = 128
TOK_DEV = 512
DOCS = 4


epsilon = 1e-05
rope_base = 10000.0


def swapped(value, axis, apart):
    mask = 2**apart
    pairs = [(source, source ^ mask) for source in range(lax.axis_size(axis))]
    return lax.ppermute(value, axis, pairs)


def head_norm(values, scales):
    centre = jnp.mean(values, axis=-1, keepdims=True)
    centred = values - centre
    spread = jnp.mean(centred * centred, axis=-1, keepdims=True)
    return centred * lax.rsqrt(spread + epsilon) * scales


def rotary(values, places):
    half_dim = values.shape[-1] // 2
    freqs = jnp.exp(
        -math.log(rope_base) * 2.0 * jnp.arange(half_dim, dtype=jnp.float32) / values.shape[-1]
    )
    angles = places.astype(jnp.float32)[:, None] * freqs[None, :]
    cosine = jnp.cos(angles)[:, None, :]
    sine_part = jnp.sin(angles)[:, None, :]
    front = values[..., :half_dim]
    back = values[..., half_dim:]
    return jnp.concatenate(
        [front * cosine - back * sine_part, back * cosine + front * sine_part], axis=-1
    )


def doc_info(doc_lengths, tokens, seq_len):
    lengths = doc_lengths.reshape(-1)
    labels = jnp.arange(lengths.shape[0], dtype=jnp.int32)
    ends = labels // DOCS * seq_len + jnp.cumsum(doc_lengths, axis=1).reshape(-1)
    starts = ends - lengths
    inside = (tokens[:, None] >= starts[None, :]) & (tokens[:, None] < ends[None, :])
    doc_ids = jnp.sum(jnp.where(inside, labels[None, :], 0), axis=1)
    first_tok = jnp.sum(jnp.where(inside, starts[None, :], 0), axis=1)
    return (doc_ids, (tokens - first_tok).astype(jnp.int32))


def placement_of(tokens, seq_devs):
    seq_len = seq_devs * TOK_DEV
    half_len = TOK_DEV // 2
    group_id = tokens // seq_len
    block_id = (tokens - group_id * seq_len) // half_len
    within_group = block_id // 2
    which_half = block_id % 2
    return ((group_id * seq_devs + within_group).astype(jnp.int32), which_half.astype(jnp.int32))


def held_tokens(devices, seq_devs):
    seq_len = seq_devs * TOK_DEV
    half_len = TOK_DEV // 2
    group_id = devices // seq_devs
    inner_index = devices % seq_devs
    first_block = 2 * inner_index
    second_block = 2 * inner_index + 1
    within = jnp.arange(half_len, dtype=jnp.int32)[None, :]
    front_rows = (group_id * seq_len + first_block * half_len)[:, None] + within
    back_rows = (group_id * seq_len + second_block * half_len)[:, None] + within
    return jnp.concatenate([front_rows, back_rows], axis=1)


def on_device(stream, norm_gain, qkv_weight, qk_gain, owner, doc_lengths):
    mod_count = lax.axis_size("mod")
    device = lax.axis_index("mod")
    seq_devs = mod_count // 8
    seq_len = seq_devs * TOK_DEV
    rows_dev, model_width = stream.shape
    columns = qk_gain.shape[2]
    heads_here = columns // HD
    text_devs = mod_count // 2
    is_image = device >= text_devs
    half_len = TOK_DEV // 2
    per_half = 3 * TOK_DEV // (4 * mod_count)
    capacity = 2 * per_half
    text_rows = TOK_DEV // 2
    owned_mask = owner == device
    owned_count = jnp.sum(owned_mask.astype(jnp.int32))
    owned = jnp.nonzero(owned_mask, size=rows_dev, fill_value=owner.shape[0] - 1)[0].astype(
        jnp.int32
    )
    usable = jnp.arange(rows_dev, dtype=jnp.int32) < owned_count
    owned_places = doc_info(doc_lengths, owned, seq_len)[1]
    sample = stream.astype(jnp.float32)
    norm_scale = jnp.where(is_image, norm_gain[1], norm_gain[0])
    normed = (
        sample * lax.rsqrt(jnp.mean(sample * sample, axis=1, keepdims=True) + epsilon) * norm_scale
    ).astype(jnp.bfloat16)
    image_target = (jnp.arange(mod_count) >= text_devs)[:, None, None, None]
    outgoing = jnp.where(image_target, qkv_weight[1][None], qkv_weight[0][None])
    full_weight = lax.all_to_all(outgoing, "mod", split_axis=0, concat_axis=1, tiled=True).reshape(
        model_width, 3 * columns
    )

    def text_work():
        text_part = jnp.dot(normed[:text_rows], full_weight, preferred_element_type=jnp.float32)
        return jnp.pad(text_part, ((0, rows_dev - text_rows), (0, 0)))

    def image_work():
        return jnp.dot(normed, full_weight, preferred_element_type=jnp.float32)

    projected = lax.cond(is_image, image_work, text_work).reshape(rows_dev, 3, heads_here, HD)
    values = projected[:, 2].astype(jnp.bfloat16)
    qk_scale = jnp.where(is_image, qk_gain[1], qk_gain[0]).reshape(2, heads_here, HD)
    queries = rotary(head_norm(projected[:, 0], qk_scale[0]), owned_places).astype(jnp.bfloat16)
    rotated_keys = rotary(head_norm(projected[:, 1], qk_scale[1]), owned_places).astype(
        jnp.bfloat16
    )
    payload = jnp.stack([queries, rotated_keys, values], axis=1).reshape(rows_dev, 3, columns)
    target, which_half = placement_of(owned, seq_devs)
    half_block = owned // half_len
    block_first = jnp.searchsorted(half_block, half_block, side="left")
    slot_in = which_half * per_half + jnp.arange(rows_dev, dtype=jnp.int32) - block_first
    send_target = jnp.where(usable, target, mod_count)
    outbound = (
        jnp.zeros((mod_count, capacity, 3, columns), jnp.bfloat16)
        .at[send_target, slot_in]
        .set(payload, mode="drop")
    )
    inbound = lax.all_to_all(outbound, "mod", split_axis=0, concat_axis=0, tiled=True)
    held = held_tokens(jnp.reshape(device, (1,)), seq_devs)[0]
    sources = owner[held]
    picks = (
        (sources[:, None] == jnp.arange(mod_count, dtype=jnp.int32)[None, :])
        .astype(jnp.int32)
        .reshape(2, half_len, mod_count)
    )
    earlier = jnp.cumsum(picks, axis=1) - picks
    rank_in_block = jnp.sum(earlier * picks, axis=2).reshape(TOK_DEV)
    arrival = jnp.arange(TOK_DEV, dtype=jnp.int32) // half_len * per_half + rank_in_block
    local_rows = inbound[sources, arrival]
    query_rows = local_rows[:, 0].reshape(TOK_DEV, heads_here, HD)
    gathered = local_rows[:, 1:]
    for level in range(seq_devs.bit_length() - 1):
        partner_part = swapped(gathered, "mod", level)
        upper_side = device // (1 << level) % 2 == 1
        low_part = jnp.where(upper_side, partner_part, gathered)
        high_part = jnp.where(upper_side, gathered, partner_part)
        gathered = jnp.concatenate([low_part, high_part], axis=0)
    group_devices = device // seq_devs * seq_devs + jnp.arange(seq_devs, dtype=jnp.int32)
    key_tokens = held_tokens(group_devices, seq_devs).reshape(-1)
    key_docs = doc_info(doc_lengths, key_tokens, seq_len)[0]
    query_docs = doc_info(doc_lengths, held, seq_len)[0]
    key_width = min(512, seq_len)
    block_total = seq_len // key_width

    def attend(block_index, totals):
        offset = block_index * key_width
        key_part = lax.dynamic_slice_in_dim(gathered, offset, key_width, 0)
        tok_part = lax.dynamic_slice_in_dim(key_tokens, offset, key_width, 0)
        doc_part = lax.dynamic_slice_in_dim(key_docs, offset, key_width, 0)
        visible = (query_docs[:, None] == doc_part[None, :]) & (tok_part[None, :] <= held[:, None])

        def compute(current):
            numerator, denominator = current
            scores = jnp.einsum(
                "qhd,khd->hqk",
                query_rows,
                key_part[:, 0].reshape(key_width, heads_here, HD),
                preferred_element_type=jnp.float32,
            ) / math.sqrt(HD)
            weights = jnp.where(visible[None], jnp.exp(scores), 0.0)
            numerator = numerator + jnp.einsum(
                "hqk,khd->qhd",
                weights.astype(jnp.bfloat16),
                key_part[:, 1].reshape(key_width, heads_here, HD),
                preferred_element_type=jnp.float32,
            )
            denominator = denominator + jnp.sum(weights, axis=2)
            return (numerator, denominator)

        return lax.cond(jnp.any(visible), compute, lambda current: current, totals)

    start_totals = (
        jnp.zeros((TOK_DEV, heads_here, HD), jnp.float32),
        jnp.zeros((heads_here, TOK_DEV), jnp.float32),
    )
    numerator, denominator = lax.fori_loop(0, block_total, attend, start_totals)
    mixed = (
        (numerator / jnp.transpose(denominator)[:, :, None])
        .astype(jnp.bfloat16)
        .reshape(TOK_DEV, columns)
    )
    outbound_back = (
        jnp.zeros((mod_count, capacity, columns), jnp.bfloat16).at[sources, arrival].set(mixed)
    )
    came_back = lax.all_to_all(outbound_back, "mod", split_axis=0, concat_axis=0, tiled=True)
    picked = came_back[jnp.clip(target, 0, mod_count - 1), jnp.clip(slot_in, 0, capacity - 1)]
    return jnp.where(usable[:, None], picked, jnp.zeros_like(picked))


def solution(mesh):
    return jax.shard_map(
        on_device,
        mesh=mesh,
        in_specs=(P("mod", None), P(), P(None, "mod", None, "tp"), P(None, None, "tp"), P(), P()),
        out_specs=P("mod", "tp"),
        check_vma=False,
    )
```

profile of v0, /device:TPU:1, one launch (start us, length us, event | category | flops | bytes accessed | tf_op | source)
XLA Modules:
  0.0 969.2 jit_solution(9283341258128985779)
XLA Ops:
  1.1 5.7 broadcast_select_fusion
  6.8 13.3 %all-to-all-start = ((bf16[64,64,3,512]{3,1,2,0:T(8,128)(2,1)}), bf16[64,64,3,512]{3,1,2,0:T(8,128)(2,1)}, u32[]{:S(2)}, u32[]{:S(2)}) async-start(bf16[64,64,3,512]{3,1,2,0:T(8,128)(2,1)} %broadcast_select_fusion), calls=%async_computation | async-start | bytes 25165824 | tf_op jit(solution)/shard_map/all_to_all | solution.py:107
  22.2 226.8 %scatter_custom_fusion = s32[768]{0:T(1024)S(1)} fusion(s32[32768]{0:T(1024)S(1)} %bitcast.139, s32[32768]{0:T(1024)S(1)} %broadcast.1035, s32[]{:T(128)} %constant.342.clone.1), kind=kCustom, calls=%fused_computation.182 | custom fusion | flops 32768 | bytes 3076 | tf_op jit(solution)/shard_map/scatter-add | solution.py:95
  250.7 32.8 %while.41 = (s32[]{:T(128)}, u32[768]{0:T(1024)S(1)}, u32[768]{0:T(1024)S(1)}, s32[768]{0:T(1024)S(1)}, s32[]{:T(128)}, /*index=5*/s32[]{:T(128)}, s32[]{}) while((s32[]{:T(128)}, u32[768]{0:T(1024)S(1)}, u32[768]{0:T(1024)S(1)}, s32[768]{0:T(1024)S(1)}, s32[]{:T(128)}, /*index=5*/s32[]{:T(128)}, s32[]{}) %tuple.114), condition=%wide.region_11.12_spmd.clone, body=%wide.region_10.11_spmd.clone.sunk | while | flops 14852 | bytes 57957 | solution.py:128
  289.4 8.2 fusion.19
  297.6 16.7 %copy.72 = bf16[64,64,3,512]{3,2,1,0:T(4,128)(2,1)S(1)} copy(bf16[64,64,3,512]{3,1,2,0:T(8,128)(2,1)} %all-to-all-done) | data formatting | bytes 25165824 | tf_op jit(solution)/shard_map/all_to_all | solution.py:107
  314.4 10.8 %copy.89 = bf16[512,8,3,512]{3,1,2,0:T(8,128)(2,1)} copy(bf16[512,8,3,512]{3,2,1,0:T(4,128)(2,1)S(1)} %bitcast.121) | data formatting | bytes 25165824
  325.2 10.0 %conditional.2 = (f32[768,1536]{1,0:T(8,128)}) conditional(s32[]{:T(128)} %convert_element_type.88, (bf16[768,4096]{1,0:T(8,128)(2,1)}, bf16[4096,1536]{1,0:T(8,128)(2,1)}) %tuple.124, (bf16[768,4096]{1,0:T(8,128)(2,1)}, bf16[4096,1536]{1,0:T(8,128)(2,1)}) %tuple.125), branch_computations={%region_13.14_spmd, %region_14.15_spmd} | conditional | flops 9663676416 | bytes 23592968 | solution.py:118
  325.2 7.1 fusion
  335.2 6.0 copy.73
  356.2 86.9 %scatter_fusion = bf16[64,12,3,512]{3,2,1,0:T(4,128)(2,1)} fusion(bf16[64,12,3,512]{3,2,1,0:T(4,128)(2,1)} %broadcast_in_dim.204, s32[768]{0:T(1024)S(1)} %get-tuple-element.343, bf16[768,3,512]{2,1,0:T(4,128)(2,1)S(1)} %copy.74), kind=kCustom, calls=%fused_computation.5 | custom fusion | bytes 7084032 | tf_op jit(solution)/shard_map/scatter | solution.py:134
  443.1 18.3 %all-to-all-start.1 = ((bf16[64,12,3,512]{3,2,1,0:T(4,128)(2,1)}), bf16[64,12,3,512]{3,2,1,0:T(4,128)(2,1)S(1)}, u32[]{:S(2)}, u32[]{:S(2)}) async-start(bf16[64,12,3,512]{3,2,1,0:T(4,128)(2,1)} %scatter_fusion), calls=%async_computation.1 | async-start | bytes 6291456 | tf_op jit(solution)/shard_map/all_to_all | solution.py:136
  466.3 68.6 %all-to-all-done.1 = bf16[64,12,3,512]{3,2,1,0:T(4,128)(2,1)S(1)} async-done(((bf16[64,12,3,512]{3,2,1,0:T(4,128)(2,1)}), bf16[64,12,3,512]{3,2,1,0:T(4,128)(2,1)S(1)}, u32[]{:S(2)}, u32[]{:S(2)}) %all-to-all-start.1) | async-done | bytes 2359328 | tf_op jit(solution)/shard_map/all_to_all | solution.py:136
  553.6 46.9 %collective-permute-done.1 = bf16[1024,2,512]{2,1,0:T(2,128)(2,1)} collective-permute-done((bf16[1024,2,512]{2,1,0:T(2,128)(2,1)S(1)}, bf16[1024,2,512]{2,1,0:T(2,128)(2,1)}, u32[]{:S(2)}, u32[]{:S(2)}) %collective-permute-start.1) | collective-permute-done | bytes 2097184 | tf_op jit(solution)/shard_map/ppermute | solution.py:20
  600.5 5.8 broadcast_select_fusion.4
  606.3 12.4 %pad_maximum_fusion.1 = bf16[2048,2,512]{2,1,0:T(2,128)(2,1)} fusion(bf16[1024,2,512]{2,1,0:T(2,128)(2,1)S(1)} %get-tuple-element.395, bf16[1024,2,512]{2,1,0:T(2,128)(2,1)S(1)} %get-tuple-element.394), kind=kLoop, calls=%fused_computation.36 | loop fusion | flops 2097152 | bytes 8388608 | tf_op jit(solution)/shard_map/concatenate | solution.py:155
  625.6 176.9 %collective-permute-done.2 = bf16[2048,2,512]{2,1,0:T(2,128)(2,1)} collective-permute-done((bf16[2048,2,512]{2,1,0:T(2,128)(2,1)}, bf16[2048,2,512]{2,1,0:T(2,128)(2,1)}, u32[]{:S(2)}, u32[]{:S(2)}) %collective-permute-start.2) | collective-permute-done | bytes 4194336 | tf_op jit(solution)/shard_map/ppermute | solution.py:20
  802.5 16.4 %broadcast_select_fusion.2 = (bf16[2048,2,512]{2,1,0:T(2,128)(2,1)S(1)}, bf16[2048,2,512]{2,1,0:T(2,128)(2,1)S(1)}) fusion(bf16[2048,2,512]{2,1,0:T(2,128)(2,1)} %collective-permute-done.2, pred[]{:T(512)S(6)} %eq.95, bf16[1024,2,512]{2,1,0:T(2,128)(2,1)} %copy-done.2, bf16[1024,2,512]{2,1,0:T(2,128)(2,1)S(1)} %get-tuple-element.394), kind=kLoop, calls=%fused_computation.35 | loop fusion | flops 6291456 | bytes 16777216 | tf_op jit(solution)/shard_map/jit(_where)/select_n | solution.py:153
  818.9 24.0 %pad_maximum_fusion = bf16[4096,2,512]{2,1,0:T(2,128)(2,1)} fusion(bf16[2048,2,512]{2,1,0:T(2,128)(2,1)S(1)} %get-tuple-element.391, bf16[2048,2,512]{2,1,0:T(2,128)(2,1)S(1)} %get-tuple-element.390), kind=kLoop, calls=%fused_computation.33 | loop fusion | flops 4194304 | bytes 16777216 | tf_op jit(solution)/shard_map/concatenate | solution.py:155
  842.9 21.3 %copy.76 = bf16[4096,2,512]{0,2,1:T(8,128)(2,1)} copy(bf16[4096,2,512]{2,1,0:T(2,128)(2,1)} %pad_maximum_fusion) | data formatting | bytes 16777216 | tf_op jit(solution)/shard_map/while | solution.py:194
  864.3 21.8 %while.40 = (s32[]{:T(128)}, f32[512,4,128]{2,0,1:T(8,128)S(1)}, f32[4,512]{1,0:T(4,128)S(1)}, s32[512]{0:T(512)S(1)}, s32[4096]{0:T(1024)S(1)}, /*index=5*/s32[...) while((s32[]{:T(128)}, f32[512,4,128]{2,0,1:T(8,128)S(1)}, ...), condition=%wide.region_29.30_spmd, body=%wide.region_24.29_spmd.sunk | while | flops 544473088 | bytes 14991653 | solution.py:194
  886.9 27.0 %scatter_fusion.1 = bf16[64,12,512]{2,0,1:T(8,128)(2,1)S(1)} fusion(bf16[64,12,512]{2,0,1:T(8,128)(2,1)S(1)} %broadcast_in_dim.197, s32[512]{0:T(512)S(1)} %bitcast.127, bf16[512,512]{1,0:T(8,128)(2,1)S(1)} %copy.79), kind=kCustom, calls=%fused_computation.6 | custom fusion | bytes 1576960 | tf_op jit(solution)/shard_map/scatter | solution.py:201
  915.3 18.0 %all-to-all-start.2 = ((bf16[64,12,512]{2,1,0:T(8,128)(2,1)}), bf16[64,12,512]{2,1,0:T(8,128)(2,1)S(1)}, u32[]{:S(2)}, u32[]{:S(2)}) async-start(bf16[64,12,512]{2,1,0:T(8,128)(2,1)} %copy.80), calls=%async_computation.2 | async-start | bytes 2097152 | tf_op jit(solution)/shard_map/all_to_all | solution.py:203
  934.0 27.8 %all-to-all-done.2 = bf16[64,12,512]{2,1,0:T(8,128)(2,1)S(1)} async-done(((bf16[64,12,512]{2,1,0:T(8,128)(2,1)}), bf16[64,12,512]{2,1,0:T(8,128)(2,1)S(1)}, u32[]{:S(2)}, u32[]{:S(2)}) %all-to-all-start.2) | async-done | bytes 786464 | tf_op jit(solution)/shard_map/all_to_all | solution.py:203
  (217 shorter events, 126.0 us)
Async XLA Ops:
  6.8 13.3 %copy-start.7 = (s32[8,4]{0,1:T(4,128)S(1)}, s32[8,4]{0,1:T(4,128)}, u32[]{:S(2)}) copy-start(s32[8,4]{0,1:T(4,128)} %param.19) | copy-start | bytes 388
  6.8 13.4 %copy-start.1 = (s32[32768]{0:T(1024)S(1)}, s32[32768]{0:T(1024)}, u32[]{:S(2)}) copy-start(s32[32768]{0:T(1024)} %param.18) | copy-start | bytes 393220
  6.8 290.8 %all-to-all-start = ((bf16[64,64,3,512]{3,1,2,0:T(8,128)(2,1)}), bf16[64,64,3,512]{3,1,2,0:T(8,128)(2,1)}, u32[]{:S(2)}, u32[]{:S(2)}) async-start(bf16[64,64,3,512]{3,1,2,0:T(8,128)(2,1)} %broadcast_select_fusion), calls=%async_computation | async-start | bytes 25165824 | tf_op jit(solution)/shard_map/all_to_all | solution.py:107
  284.4 4.1 copy-start.8
  284.5 4.9 copy-start.6
  341.2 3.9 copy-start
  443.1 91.8 %all-to-all-start.1 = ((bf16[64,12,3,512]{3,2,1,0:T(4,128)(2,1)}), bf16[64,12,3,512]{3,2,1,0:T(4,128)(2,1)S(1)}, u32[]{:S(2)}, u32[]{:S(2)}) async-start(bf16[64,12,3,512]{3,2,1,0:T(4,128)(2,1)} %scatter_fusion), calls=%async_computation.1 | async-start | bytes 6291456 | tf_op jit(solution)/shard_map/all_to_all | solution.py:136
  534.9 1.7 copy-start.5
  541.8 7.7 copy-start.3
  542.9 3.1 collective-permute-start
  549.6 1.0 copy-start.4
  553.2 47.2 %collective-permute-start.1 = (bf16[1024,2,512]{2,1,0:T(2,128)(2,1)S(1)}, bf16[1024,2,512]{2,1,0:T(2,128)(2,1)}, u32[]{:S(2)}, u32[]{:S(2)}) collective-permute-start(bf16[1024,2,512]{2,1,0:T(2,128)(2,1)S(1)} %pad_maximum_fusion.3), channel_id=1, source_target_pairs={{0,8},{4,12},{8,0},{12,4},{16,24},{20,28},{24,16},{28,20},{32,40},... | collective-permute-start | bytes 6291464 | tf_op jit(solution)/shard_map/ppermute | solution.py:20
  606.3 12.4 %copy-start.2 = (bf16[1024,2,512]{2,1,0:T(2,128)(2,1)}, bf16[1024,2,512]{2,1,0:T(2,128)(2,1)S(1)}, u32[]{:S(2)}) copy-start(bf16[1024,2,512]{2,1,0:T(2,128)(2,1)S(1)} %get-tuple-element.395) | copy-start | bytes 6291460
  618.7 183.8 %collective-permute-start.2 = (bf16[2048,2,512]{2,1,0:T(2,128)(2,1)}, bf16[2048,2,512]{2,1,0:T(2,128)(2,1)}, u32[]{:S(2)}, u32[]{:S(2)}) collective-permute-start(bf16[2048,2,512]{2,1,0:T(2,128)(2,1)} %pad_maximum_fusion.1), channel_id=1, source_target_pairs={{0,16},{4,20},{8,24},{12,28},{16,0},{20,4},{24,8},{28,12},{32,48},... | collective-permute-start | bytes 12582920 | tf_op jit(solution)/shard_map/ppermute | solution.py:20
  915.3 46.5 %all-to-all-start.2 = ((bf16[64,12,512]{2,1,0:T(8,128)(2,1)}), bf16[64,12,512]{2,1,0:T(8,128)(2,1)S(1)}, u32[]{:S(2)}, u32[]{:S(2)}) async-start(bf16[64,12,512]{2,1,0:T(8,128)(2,1)} %copy.80), calls=%async_computation.2 | async-start | bytes 2097152 | tf_op jit(solution)/shard_map/all_to_all | solution.py:203
where the time goes:
time: 977 us; the launch traced here: 969 us
  other arithmetic  331 us (34%)
  waiting for transfers between devices  323 us (33%)
  local copies, waits for them, and re-layouts  245 us (25%)
  starting transfers between devices  50.8 us (5%)
  matrix products  12.8 us (1%)
    scatter-add x1, other arithmetic, on_device(): jnp.nonzero(owned_mask, size=rows_dev, fill_value=owner.shape[0] - 1)[0]  227 us
    ppermute x3, waiting for transfers between devices, swapped(): return lax.ppermute(value, axis, pairs)  227 us
    scatter x1, local copies, waits for them, and re-layouts, on_device(): outbound = jnp.zeros((mod_count, capacity, 3, columns), jnp.bfloat16).at[...  86.9 us
    all_to_all x1, waiting for transfers between devices, on_device(): lax.all_to_all(outbound, 'mod', split_axis=0, concat_axis=0, tiled=True)  68.6 us
    concatenate x3, other arithmetic, on_device(): gathered = jnp.concatenate([low_part, high_part], axis=0)  39.1 us
    gather x10, local copies, waits for them, and re-layouts, on_device(): block_first = jnp.searchsorted(half_block, half_block, side='left')  31.9 us
    scatter x2, local copies, waits for them, and re-layouts, on_device(): jnp.zeros((mod_count, capacity, columns), jnp.bfloat16).at[sources, arrival]  28.4 us
    all_to_all x1, waiting for transfers between devices, on_device(): lax.all_to_all(outbound_back, 'mod', split_axis=0, concat_axis=0, tiled=T...  27.8 us
  transfers between devices with their start and end apart: 6, of which 5 were waited for; matrix products, arithmetic and copies ran while one was open for 30% of the time, Pallas kernels for 0%

commit v1 on v0

v1 whole, which is shorter than its diff:
```python
import math

import jax
import jax.numpy as jnp
import numpy as np
from jax import lax
from jax.experimental import pallas as pl
from jax.experimental.pallas import tpu as pltpu
from jax.sharding import PartitionSpec as P

HD = 128
BLOCK = 256
SEQ_LEN = 4096
SEQS = 8
BLOCKS = 128
ROWS = 768
TEXT_ROWS = 256
XS = 4
ZS = 8
CHIPS = XS * ZS
HEADS = 4
WIDTH = HEADS * HD
MODEL = 4096
K_CHUNK = 64
TEXT_CHIPS = CHIPS // 2
TEXT_HALF = 16
IMAGE_HALF = 48
PART = TEXT_CHIPS * (TEXT_HALF + IMAGE_HALF)
Q_TILE = 256
MESH = pl.DeviceIdType.MESH

epsilon = 1e-05
rope_base = 10000.0


def place_of():
    me = lax.axis_index("mod")
    core = lax.rem(me, 2)
    chip = lax.div(me, 2)
    return lax.div(chip, ZS), lax.rem(chip, ZS), core, lax.axis_index("tp")


def project_kernel(
    w_ref, x_ref, gain_ref, cos_ref, sin_ref, qk_ref, out_ref,
    weights, rows, normed, acc,
    z_send, z_recv, x_send, x_recv, s_send, s_recv, c_send, c_recv, load_sem, own_sem,
):
    x, z, core, tp = place_of()
    modality = lax.div(x, 2)
    x_in = x + 1 - 2 * lax.rem(x, 2)
    columns = (x, 3 - x, 3 - x_in)

    def device(xx, zz, cc):
        return ((xx * ZS + zz) * 2 + cc, tp)

    def around(steps):
        return lax.rem(z + steps + 2 * ZS, ZS)

    z_next = (device(x, around(1), core), device(x, around(-1), core))
    partner = device(x_in, z, core)
    across = device(3 - x, z, core)
    sibling = device(x, z, 1 - core)

    def put(src, dst, send, recv, target):
        return pltpu.make_async_remote_copy(
            src_ref=src, dst_ref=dst, send_sem=send, recv_sem=recv,
            device_id=target, device_id_type=MESH,
        )

    def spot(zz, xx):
        return weights.at[zz, :, xx, core]

    def along_z(kind, way, hop, src=None):
        zz = around((1 - hop) if way == 0 else (hop - 1))
        here = spot(zz, columns[kind])
        return put(
            here if src is None else src, here,
            z_send.at[kind, way, hop - 1], z_recv.at[kind, way, hop - 1], z_next[way],
        )

    def to_partner(slot, zz, xx, src=None):
        here = spot(zz, xx)
        return put(here if src is None else src, here, x_send.at[slot], x_recv.at[slot], partner)

    def to_sibling(zz, xx, src=None):
        here = spot(zz, xx)
        return put(
            here if src is None else src, here, s_send.at[zz, xx], s_recv.at[zz, xx], sibling
        )

    def long_way(kind):
        return lax.rem(kind + core, 2)

    barrier = pltpu.get_barrier_semaphore()
    for target in (z_next[0], z_next[1], partner, across, sibling):
        pl.semaphore_signal(barrier, inc=1, device_id=target, device_id_type=MESH)
    pl.semaphore_wait(barrier, 5)

    mine = w_ref.at[modality]
    cross = put(w_ref.at[1 - modality], spot(z, x), c_send, c_recv, across)
    cross.start()
    for way in range(2):
        along_z(0, way, 1, mine).start()
    to_partner(z, z, x, mine).start()
    to_sibling(z, x, mine).start()
    own = pltpu.make_async_copy(mine, spot(z, x), own_sem)
    own.start()
    pieces = [
        pltpu.make_async_copy(
            x_ref.at[pl.ds(i * 128, 128)], rows.at[pl.ds(i * 128, 128)], load_sem.at[i]
        )
        for i in range(ROWS // 128)
    ]
    for piece in pieces:
        piece.start()

    def normalize(i):
        pieces[i].wait()

        @pl.loop(0, 8)
        def _(group):
            at = pl.multiple_of(i * 128 + group * 16, 16)
            sample = rows[pl.ds(at, 16), :].astype(jnp.float32)
            scale = lax.rsqrt(jnp.mean(sample * sample, axis=1, keepdims=True) + epsilon)
            scaled = (sample * scale * gain_ref[pl.ds(modality, 1), :]).astype(jnp.bfloat16)
            for zz in range(ZS):
                for xx in range(XS):
                    k = (xx * ZS + zz) * 128
                    normed[zz, pl.ds(at, 16), xx * 128 : xx * 128 + 128] = scaled[:, k : k + 128]

    normalize(0)
    normalize(1)
    put(w_ref.at[modality], spot(z, 3 - x), c_send, c_recv, across).wait_recv()
    to_partner(ZS, z, 3 - x).start()
    for way in range(2):
        along_z(1, way, 1).start()
    to_sibling(z, 3 - x).start()
    normalize(2)
    normalize(3)
    to_partner(ZS, z, 3 - x_in).wait_recv()
    for way in range(2):
        along_z(2, way, 1).start()
    to_sibling(z, 3 - x_in).start()
    to_partner(z, z, x_in).wait_recv()
    to_sibling(z, x_in).start()
    normalize(4)
    normalize(5)
    own.wait()

    def arrive(kind, way, hop, last):
        zz = around(-hop if way == 0 else hop)
        along_z(kind, way, hop).wait_recv()
        if not last:
            onward = jnp.logical_or(hop < 3, long_way(kind) == way)

            @pl.when(onward)
            def _():
                along_z(kind, way, hop + 1).start()

        if kind == 0:
            to_partner(zz, zz, x).start()
        to_sibling(zz, columns[kind]).start()

    def from_partner(zz):
        to_partner(zz, zz, x_in).wait_recv()
        to_sibling(zz, x_in).start()

    def consume(zz, first=False):
        for xx in range(XS):
            to_sibling(zz, xx).wait_recv()
        lhs = normed[zz]
        for j in range(3):
            part = jnp.dot(
                lhs, weights[zz, j].reshape(XS * 2 * K_CHUNK, WIDTH),
                preferred_element_type=jnp.float32,
            )
            if first:
                acc[j] = part
            else:
                acc[j] += part

    def hop_step(hop, first):
        for kind in range(3):
            for way in range(2):
                arrive(kind, way, hop, False)
        for way in range(2):
            from_partner(around(-hop if way == 0 else hop))
        if first:
            consume(z, True)

    hop_step(1, True)

    @pl.loop(2, 4)
    def _(hop):
        hop_step(hop, False)

        @pl.loop(0, 2)
        def _(way):
            consume(around((hop - 1) * (2 * way - 1)))

    @pl.loop(0, 2)
    def _(way):
        consume(around(3 * (2 * way - 1)))

    far = around(4)
    for kind in range(3):
        for way in range(2):

            @pl.when(long_way(kind) == way)
            def _():
                arrive(kind, way, 4, True)

    from_partner(far)
    consume(far)

    @pl.loop(0, ROWS // 128)
    def _(i):
        at = pl.ds(pl.multiple_of(i * 128, 128), 128)
        cosine = cos_ref[at, :]
        sine = sin_ref[at, :]
        for head in range(HEADS):
            lanes = slice(head * HD, head * HD + HD)
            for j in range(2):
                value = acc[j, at, lanes]
                centred = value - jnp.mean(value, axis=-1, keepdims=True)
                spread = jnp.mean(centred * centred, axis=-1, keepdims=True)
                scaled = centred * lax.rsqrt(spread + epsilon) * qk_ref[modality, pl.ds(j, 1), lanes]
                turned = scaled * cosine + pltpu.roll(scaled, HD // 2, 1) * sine
                out_ref[head, j, at, :] = turned.astype(jnp.bfloat16)
            out_ref[head, 2, at, :] = acc[2, at, lanes].astype(jnp.bfloat16)

    cross.wait_send()
    for kind in range(3):
        for way in range(2):
            for hop in range(1, 4):
                along_z(kind, way, hop).wait_send()

            @pl.when(long_way(kind) == way)
            def _():
                along_z(kind, way, 4).wait_send()

    for slot in range(ZS):
        to_partner(slot, slot, x).wait_send()
    to_partner(ZS, z, x).wait_send()
    for zz in range(ZS):
        for xx in range(XS):
            to_sibling(zz, xx).wait_send()


def project(w, stream, gain, cosines, sines, qk):
    vmem = pl.BlockSpec(memory_space=pltpu.VMEM)
    dma = pltpu.SemaphoreType.DMA
    return pl.pallas_call(
        project_kernel,
        name="gather_project",
        out_shape=jax.ShapeDtypeStruct((HEADS, 3, ROWS, HD), jnp.bfloat16),
        in_specs=[vmem, pl.BlockSpec(memory_space=pl.ANY), vmem, vmem, vmem, vmem],
        out_specs=vmem,
        scratch_shapes=[
            pltpu.VMEM((ZS, 3, XS, 2, K_CHUNK, WIDTH), jnp.bfloat16),
            pltpu.VMEM((ROWS, MODEL), jnp.bfloat16),
            pltpu.VMEM((ZS, ROWS, XS * 128), jnp.bfloat16),
            pltpu.VMEM((3, ROWS, WIDTH), jnp.float32),
            dma((3, 2, 4)), dma((3, 2, 4)),
            dma((ZS + 1,)), dma((ZS + 1,)),
            dma((ZS, XS)), dma((ZS, XS)),
            dma, dma,
            dma((ROWS // 128,)), dma,
        ],
        compiler_params=pltpu.CompilerParams(
            collective_id=0, has_side_effects=True, vmem_limit_bytes=60 << 20
        ),
    )(w, stream, gain, cosines, sines, qk)


def attend_kernel(
    pay_ref, kpos_ref, qpos_ref, qstart_ref, out_ref,
    held, num, den, mixed, blank,
    a_send, a_recv, s_send, s_recv, b_send, b_recv, zero_sem,
):
    x, z, core, tp = place_of()
    me = x * ZS + z
    seq, head = lax.div(me, HEADS), lax.rem(me, HEADS)
    is_image = x >= XS // 2
    sibling = (2 * me + 1 - core, tp)

    def chip(steps):
        return lax.rem(me + steps + CHIPS, CHIPS)

    barrier = pltpu.get_barrier_semaphore()

    @pl.loop(1, CHIPS)
    def _(i):
        pl.semaphore_signal(
            barrier, inc=1, device_id=(2 * chip(i) + core, tp), device_id_type=MESH
        )

    pl.semaphore_signal(barrier, inc=1, device_id=sibling, device_id_type=MESH)
    pl.semaphore_wait(barrier, CHIPS)

    def outbound(to, image, part):
        size = IMAGE_HALF if image else TEXT_HALF
        at = pl.multiple_of((2 * lax.div(to, HEADS) + part) * size, 16)
        return pay_ref.at[lax.rem(to, HEADS), :, pl.ds(at, size)]

    def landing(source, image, part):
        if image:
            at = TEXT_CHIPS * TEXT_HALF + (source - TEXT_CHIPS) * IMAGE_HALF
            size = IMAGE_HALF
        else:
            at = source * TEXT_HALF
            size = TEXT_HALF
        return pl.ds(pl.multiple_of(at, 16), size)

    def forth(to, image, part, target):
        return pltpu.make_async_remote_copy(
            src_ref=outbound(to, image, part),
            dst_ref=held.at[:, part, core, landing(me, image, part)],
            send_sem=a_send.at[to], recv_sem=a_recv.at[me],
            device_id=target, device_id_type=MESH,
        )

    def both(test, do):
        @pl.when(test)
        def _():
            do(True)

        @pl.when(jnp.logical_not(test))
        def _():
            do(False)

    def start_self(image):
        for part in range(2):
            pltpu.make_async_copy(
                outbound(me, image, part),
                held.at[:, part, core, landing(me, image, part)],
                a_recv.at[me],
            ).start()

    both(is_image, start_self)

    @pl.loop(1, CHIPS)
    def _(i):
        to = chip(i)

        def start(image):
            for part in range(2):
                forth(to, image, part, (2 * to + core, tp)).start()

        both(is_image, start)

    @pl.when(jnp.logical_not(is_image))
    def _():
        blank[...] = jnp.zeros_like(blank)
        pltpu.make_async_copy(blank, out_ref.at[pl.ds(TEXT_ROWS, ROWS - TEXT_ROWS)], zero_sem).start()

    @pl.loop(0, CHIPS)
    def _(i):
        source = chip(-i)

        def arrive(image):
            size = 2 * (IMAGE_HALF if image else TEXT_HALF)
            whole = pay_ref.at[0, :, pl.ds(0, size)]
            pltpu.make_async_copy(whole, whole, a_recv.at[source]).wait()

        both(source >= TEXT_CHIPS, arrive)

    def share(part):
        mine = held.at[pl.ds(1, 2), part, core]
        return pltpu.make_async_remote_copy(
            src_ref=mine, dst_ref=mine, send_sem=s_send.at[part], recv_sem=s_recv.at[part],
            device_id=sibling, device_id_type=MESH,
        )

    def shared(part):
        other = held.at[pl.ds(1, 2), part, 1 - core]
        return pltpu.make_async_remote_copy(
            src_ref=other, dst_ref=other, send_sem=s_send.at[part], recv_sem=s_recv.at[part],
            device_id=sibling, device_id_type=MESH,
        )

    share(0).start()
    share(1).start()

    def attend(side, first):
        @pl.loop(0, 2 * PART // Q_TILE)
        def _(tile):
            part = lax.div(tile, PART // Q_TILE)
            at = pl.ds(
                pl.multiple_of(lax.rem(tile, PART // Q_TILE) * Q_TILE, Q_TILE), Q_TILE
            )
            query = held[0, part, core, at, :]
            place = qpos_ref[part, at, :]
            start = qstart_ref[part, at, :]

            def step(key_part, fresh):
                keys = held[1, key_part, side]
                values = held[2, key_part, side]
                scores = lax.dot_general(
                    query, keys, (((1,), (1,)), ((), ())), preferred_element_type=jnp.float32
                )
                spots = kpos_ref[key_part, side]
                visible = (spots <= place) & (spots >= start)
                weight = jnp.where(visible, jnp.exp(scores * (1.0 / math.sqrt(HD))), 0.0)
                total = jnp.sum(weight, axis=1, keepdims=True)
                product = jnp.dot(
                    weight.astype(jnp.bfloat16), values, preferred_element_type=jnp.float32
                )
                if fresh:
                    num[part, at, :] = product
                    den[part, at, :] = jnp.broadcast_to(total, product.shape)
                else:
                    num[part, at, :] += product
                    den[part, at, :] += jnp.broadcast_to(total, product.shape)

            step(0, first)

            @pl.when(part == 1)
            def _():
                step(1, False)

    attend(core, True)
    shared(0).wait_recv()
    shared(1).wait_recv()
    attend(1 - core, False)

    @pl.loop(0, 2 * PART // Q_TILE)
    def _(tile):
        part = lax.div(tile, PART // Q_TILE)
        at = pl.ds(pl.multiple_of(lax.rem(tile, PART // Q_TILE) * Q_TILE, Q_TILE), Q_TILE)
        mixed[part, at, :] = (num[part, at, :] / den[part, at, :]).astype(jnp.bfloat16)

    def home(image, part, who_seq, who_head):
        size = IMAGE_HALF if image else TEXT_HALF
        at = pl.multiple_of((2 * who_seq + part) * size, 16)
        return out_ref.at[pl.ds(at, size), pl.ds(pl.multiple_of(who_head * HD, HD), HD)]

    def back(to, image, part):
        return pltpu.make_async_remote_copy(
            src_ref=mixed.at[part, landing(to, image, part)],
            dst_ref=home(image, part, seq, head),
            send_sem=b_send.at[to], recv_sem=b_recv.at[me],
            device_id=(2 * to + core, tp), device_id_type=MESH,
        )

    @pl.loop(1, CHIPS)
    def _(i):
        to = chip(i)

        def start(image):
            for part in range(2):
                back(to, image, part).start()

        both(to >= TEXT_CHIPS, start)

    def back_self(image):
        for part in range(2):
            pltpu.make_async_copy(
                mixed.at[part, landing(me, image, part)],
                home(image, part, seq, head), b_recv.at[me],
            ).start()

    both(is_image, back_self)

    @pl.loop(0, CHIPS)
    def _(i):
        source = chip(-i)

        def arrive(image):
            size = 2 * (IMAGE_HALF if image else TEXT_HALF)
            whole = mixed.at[0, pl.ds(0, size)]
            pltpu.make_async_copy(whole, whole, b_recv.at[source]).wait()

        both(is_image, arrive)

    @pl.loop(1, CHIPS)
    def _(i):
        to = chip(i)

        def sent(image):
            size = 2 * (IMAGE_HALF if image else TEXT_HALF)
            whole = pay_ref.at[0, :, pl.ds(0, size)]
            pltpu.make_async_copy(whole, whole, a_send.at[to]).wait()

        both(is_image, sent)

        def returned(image):
            size = 2 * (IMAGE_HALF if image else TEXT_HALF)
            whole = mixed.at[0, pl.ds(0, size)]
            pltpu.make_async_copy(whole, whole, b_send.at[to]).wait()

        both(to >= TEXT_CHIPS, returned)

    share(0).wait_send()
    share(1).wait_send()

    @pl.when(jnp.logical_not(is_image))
    def _():
        pltpu.make_async_copy(blank, out_ref.at[pl.ds(TEXT_ROWS, ROWS - TEXT_ROWS)], zero_sem).wait()


def attend_all(payload, key_places, query_places, query_starts):
    vmem = pl.BlockSpec(memory_space=pltpu.VMEM)
    dma = pltpu.SemaphoreType.DMA
    return pl.pallas_call(
        attend_kernel,
        name="exchange_attend",
        out_shape=jax.ShapeDtypeStruct((ROWS, WIDTH), jnp.bfloat16),
        in_specs=[vmem, vmem, vmem, vmem],
        out_specs=pl.BlockSpec(memory_space=pl.ANY),
        scratch_shapes=[
            pltpu.VMEM((3, 2, 2, PART, HD), jnp.bfloat16),
            pltpu.VMEM((2, PART, HD), jnp.float32),
            pltpu.VMEM((2, PART, HD), jnp.float32),
            pltpu.VMEM((2, PART, HD), jnp.bfloat16),
            pltpu.VMEM((ROWS - TEXT_ROWS, WIDTH), jnp.bfloat16),
            dma((CHIPS,)), dma((CHIPS,)),
            dma((2,)), dma((2,)),
            dma((CHIPS,)), dma((CHIPS,)),
            dma,
        ],
        compiler_params=pltpu.CompilerParams(
            collective_id=1, has_side_effects=True, vmem_limit_bytes=60 << 20
        ),
    )(payload, key_places, query_places, query_starts)


def doc_starts(doc_lengths):
    return jnp.cumsum(doc_lengths, axis=1) - doc_lengths


def owned_tokens(owner, device, is_image):
    by_block = owner.reshape(BLOCKS, BLOCK)
    mask = by_block == device
    order = np.arange(BLOCK)
    before = jnp.asarray(order[:, None] < order[None, :], jnp.bfloat16)
    rank = jnp.dot(mask.astype(jnp.bfloat16), before, preferred_element_type=jnp.float32)
    tokens = jnp.arange(owner.shape[0], dtype=jnp.int32).reshape(BLOCKS, 1, BLOCK)
    wanted = jnp.arange(6, dtype=jnp.int32).astype(jnp.float32)[None, :, None]
    hit = mask[:, None, :] & (rank[:, None, :] == wanted)
    found = jnp.sum(jnp.where(hit, tokens, 0), axis=2)
    image = found.reshape(ROWS)
    text = jnp.pad(found[:, :2].reshape(TEXT_ROWS), (0, ROWS - TEXT_ROWS))
    return jnp.where(is_image, image, text)


def arrival_codes():
    codes = np.zeros((2, PART), np.int32)
    for core in range(2):
        at = 0
        for chip in range(CHIPS):
            each = 2 if chip < TEXT_CHIPS else 6
            for block in range(8):
                for rank in range(each):
                    codes[core, at] = (block * 64 + 2 * chip + core) * 8 + rank
                    at += 1
    return codes


def arrival_places(owner, seq):
    mine = lax.dynamic_slice_in_dim(owner, seq * SEQ_LEN, SEQ_LEN).reshape(16, BLOCK)
    order = jnp.arange(BLOCK, dtype=jnp.int32)
    same = (mine[:, :, None] == mine[:, None, :]) & (order[None, None, :] < order[None, :, None])
    rank = jnp.sum(same.astype(jnp.int32), axis=2)
    block = jnp.arange(16, dtype=jnp.int32)[:, None] % 8
    code = ((block * 64 + mine) * 8 + rank).reshape(2, SEQ_LEN // 2)
    places = jnp.arange(SEQ_LEN, dtype=jnp.int32).reshape(2, SEQ_LEN // 2)
    hit = code[:, None, None, :] == jnp.asarray(arrival_codes())[None, :, :, None]
    return jnp.sum(jnp.where(hit, places[:, None, None, :], 0), axis=3)


def on_device(stream, norm_gain, qkv_weight, qk_gain, owner, doc_lengths):
    device = lax.axis_index("mod")
    core = device % 2
    seq = device // 2 // HEADS
    is_image = device >= 32
    starts = doc_starts(doc_lengths)

    tokens = owned_tokens(owner, device, is_image)
    absolute = (starts + jnp.arange(SEQS, dtype=jnp.int32)[:, None] * SEQ_LEN).reshape(-1)
    first = jnp.max(jnp.where(absolute[None, :] <= tokens[:, None], absolute[None, :], 0), axis=1)
    half = jnp.arange(HD, dtype=jnp.int32) % (HD // 2)
    freqs = jnp.exp(-math.log(rope_base) * 2.0 * half.astype(jnp.float32) / HD)
    angles = (tokens - first).astype(jnp.float32)[:, None] * freqs[None, :]
    sign = jnp.where(jnp.arange(HD) < HD // 2, -1.0, 1.0).astype(jnp.float32)
    cosines = jnp.cos(angles)
    sines = jnp.sin(angles) * sign[None, :]

    key_places = arrival_places(owner, seq)
    seq_starts = lax.dynamic_slice_in_dim(starts, seq, 1, 0)[0]
    query_places = lax.dynamic_slice_in_dim(key_places, core, 1, 1)[:, 0]
    query_starts = jnp.max(
        jnp.where(seq_starts <= query_places[..., None], seq_starts, 0), axis=-1
    )

    payload = project(
        jnp.transpose(qkv_weight, (0, 2, 1, 3)), stream, norm_gain, cosines, sines, qk_gain
    )
    return attend_all(
        payload, key_places[:, :, None, :], query_places[..., None], query_starts[..., None]
    )


def solution(mesh):
    return jax.shard_map(
        on_device,
        mesh=mesh,
        in_specs=(P("mod", None), P(), P(None, "mod", None, "tp"), P(None, None, "tp"), P(), P()),
        out_specs=P("mod", "tp"),
        check_vma=False,
    )
```

time: 977 us -> 187 us (0.19)
  waiting for transfers between devices: 323 us -> 0 us
  other arithmetic: 331 us -> 10.9 us
  local copies, waits for them, and re-layouts: 245 us -> 7.12 us
  Pallas kernels: 0 us -> 167 us
  starting transfers between devices: 50.8 us -> 0 us
  matrix products: 12.8 us -> 1.07 us
    scatter-add x1 -> x0, other arithmetic: 227 us -> none  [on_device(): jnp.nonzero(owned_mask, size=rows_dev, fill_value=owner.shape[0] - 1)[0]]
    ppermute x3 -> x0, waiting for transfers between devices: 227 us -> none  [swapped(): return lax.ppermute(value, axis, pairs)]
    pallas_call x0 -> x2, Pallas kernels: none -> 167 us  [the longest x1 91 us: attend_all(): pl.pallas_call(attend_kernel, name='exchange_attend', out_shape=jax.Shape...]
    scatter x3 -> x0, local copies, waits for them, and re-layouts: 115 us -> none  [the longest x1 86.9 us: on_device(): outbound = jnp.zeros((mod_count, capacity, 3, columns), jnp.bfloat16).at[...]
    all_to_all x3 -> x0, waiting for transfers between devices: 96.4 us -> none  [the longest x1 68.6 us: on_device(): lax.all_to_all(outbound, 'mod', split_axis=0, concat_axis=0, tiled=True)]
    all_to_all x3 -> x0, starting transfers between devices: 49.6 us -> none  [the longest x1 18.3 us: on_device(): lax.all_to_all(outbound, 'mod', split_axis=0, concat_axis=0, tiled=True)]
    gather x13 -> x0, local copies, waits for them, and re-layouts: 45.7 us -> none  [the longest x10 31.9 us: on_device(): block_first = jnp.searchsorted(half_block, half_block, side='left')]
    concatenate x9 -> x0, other arithmetic: 40.5 us -> none  [the longest x3 39.1 us: on_device(): gathered = jnp.concatenate([low_part, high_part], axis=0)]
  transfers between devices with their start and end apart: 6 -> 0, of which waited for: 5 -> 0; matrix products, arithmetic and copies ran while one was open for 30% -> 0% of each run, Pallas kernels for 0% -> 0%
where the time goes in v1:
time: 187 us
  Pallas kernels  167 us (89%)
  other arithmetic  10.9 us (6%)
  local copies, waits for them, and re-layouts  7.12 us (4%)
    pallas_call x1, Pallas kernels, attend_all(): pl.pallas_call(attend_kernel, name='exchange_attend', out_shape=jax.Shape...  91 us
    pallas_call x1, Pallas kernels, project(): pl.pallas_call(project_kernel, name='gather_project', out_shape=jax.Shape...  76.4 us
    reduce_sum x1, other arithmetic, arrival_places(): return jnp.sum(jnp.where(hit, places[:, None, None, :], 0), axis=3)  4.12 us

profile of v1, /device:TPU:1, one launch (start us, length us, event | category | flops | bytes accessed | tf_op | source)
XLA Modules:
  0.0 186.6 jit_solution(3805116538543479027)
XLA Ops:
  0.0 0.7 reduce_window_sum.11
  0.7 0.7 broadcast_add_fusion
  1.4 0.2 dynamic-slice_reduce_fusion
  1.6 0.1 copy.15
  1.7 0.1 le.32
  1.9 0.7 dynamic_slice.9
  2.6 0.9 broadcast_compare_fusion
  3.6 1.3 convert_reduce_fusion
  5.0 4.1 %select_reduce_fusion = s32[2,2,1024]{2,1,0:T(2,128)S(1)} fusion(s32[2,2048]{1,0:T(2,128)S(1)} %get-tuple-element.13, s32[2,1024]{1,0:T(2,128)} %constant.111.clone, s32[2,2048]{1,0:T(2,128)S(1)} %get-tuple-element.14), kind=kLoop, calls=%fused_computation | loop fusion | flops 25161728 | bytes 57344 | tf_op jit(solution)/shard_map/reduce_sum | solution.py:569
  9.1 0.6 broadcast_in_dim.73.kpos_ref
  9.8 0.1 select_reduce_fusion.3
  9.9 1.1 fusion.6
  11.0 0.3 select_reduce_fusion.1
  11.3 0.1 copy.13
  11.4 0.1 reshape.143
  11.5 0.1 copy.14
  11.6 0.1 reshape.144
  11.8 0.1 select_reduce_fusion.2
  11.9 2.5 %fusion = (f32[768,128]{1,0:T(8,128)}, f32[768,128]{1,0:T(8,128)}) fusion(f32[128]{0:T(128)S(1)} %get-tuple-element.11, f32[128]{0:T(128)S(1)} %get-tuple-element.12, f32[768]{0:T(1024)S(1)} %subtract_convert_fusion), kind=kLoop, calls=%fused_computation.5 | loop fusion | flops 196608 | bytes 790528 | tf_op jit(solution)/shard_map/mul | solution.py:587
  14.4 1.4 copy.17.qstart_ref
  15.8 1.3 broadcast_in_dim_squeeze.6.qpos_ref
  17.1 76.4 %gather_project.1.pay_ref = bf16[4,3,768,128]{3,2,1,0:T(8,128)(2,1)} custom-call(bf16[2,3,64,512]{3,2,1,0:T(8,128)(2,1)} %bitcast.10, bf16[768,4096]{1,0:T(8,128)(2,1)} %x_ref.1, f32[2,4096]{1,0:T(2,128)} %gain_ref.1, f32[768,128]{1,0:T(8,128)} %get-tuple-element.10.cos_ref, f32[768,128]{1,0:T(8,128)} %get-tuple-element.9.sin_ref, f32[2,2,512]{2,1,0:T(2,128)} %qk_ref.1), custom_call_target="tpu_custom_call" | custom-call | tf_op jit(solution)/shard_map/gather_project/pallas_call | solution.py:253
  93.5 91.0 %exchange_attend.1 = bf16[768,512]{1,0:T(8,128)(2,1)} custom-call(bf16[4,3,768,128]{3,2,1,0:T(8,128)(2,1)} %gather_project.1.pay_ref, s32[2,2,1,1024]{3,2,1,0:T(1,128)} %broadcast_in_dim.73.kpos_ref, s32[2,1024,1]{2,1,0:T(8,128)} %broadcast_in_dim_squeeze.6.qpos_ref, s32[2,1024,1]{2,1,0:T(8,128)} %copy.17.qstart_ref), custom_call_target="tpu_custom_call" | custom-call | tf_op jit(solution)/shard_map/exchange_attend/pallas_call | solution.py:505
  184.5 2.1 %copy.23 = bf16[768,512]{1,0:T(8,128)(2,1)} copy(bf16[768,512]{1,0:T(8,128)(2,1)} %exchange_attend.1) | data formatting | bytes 1572864
  (18 shorter events, 0.3 us)

commit v2 on v1

--- a/solution.py
+++ b/solution.py
@@ -275,8 +275,8 @@
 
 def attend_kernel(
     pay_ref, kpos_ref, qpos_ref, qstart_ref, out_ref,
-    held, num, den, mixed, blank,
-    a_send, a_recv, s_send, s_recv, b_send, b_recv, zero_sem,
+    held, relay, num, den, mixed, blank,
+    a_send, a_recv, r_send, r_recv, s_send, s_recv, b_send, b_recv, zero_sem,
 ):
     x, z, core, tp = place_of()
     me = x * ZS + z
@@ -312,12 +312,10 @@
             size = TEXT_HALF
         return pl.ds(pl.multiple_of(at, 16), size)
 
-    def forth(to, image, part, target):
+    def send(src, dst, send_sem, recv_sem, to):
         return pltpu.make_async_remote_copy(
-            src_ref=outbound(to, image, part),
-            dst_ref=held.at[:, part, core, landing(me, image, part)],
-            send_sem=a_send.at[to], recv_sem=a_recv.at[me],
-            device_id=target, device_id_type=MESH,
+            src_ref=src, dst_ref=dst, send_sem=send_sem, recv_sem=recv_sem,
+            device_id=(2 * to + core, tp), device_id_type=MESH,
         )
 
     def both(test, do):
@@ -339,20 +337,75 @@
 
     both(is_image, start_self)
 
-    @pl.loop(1, CHIPS)
-    def _(i):
-        to = chip(i)
+    def far_first(i):
+        return lax.rem(z + ZS // 2 + lax.div(i, 2) - lax.rem(i, 2) * (1 + 2 * lax.div(i, 2)), ZS)
+
+    @pl.loop(0, ZS - 1)
+    def _(i):
+        zz = far_first(i)
 
         def start(image):
+            size = IMAGE_HALF if image else TEXT_HALF
             for part in range(2):
-                forth(to, image, part, (2 * to + core, tp)).start()
+                to = x * ZS + zz
+                send(
+                    outbound(to, image, part), held.at[:, part, core, landing(me, image, part)],
+                    a_send.at[0, zz], a_recv.at[me], to,
+                ).start()
+            for dx in (1, 3, 2):
+                to = lax.rem(x + dx, XS) * ZS + z
+                rows = pl.ds(
+                    pl.multiple_of(
+                        2 * lax.div(lax.rem(x + dx, XS) * ZS + zz, HEADS) * size, 16
+                    ),
+                    2 * size,
+                )
+                send(
+                    pay_ref.at[lax.rem(zz, HEADS), :, rows],
+                    relay.at[x, zz, :, pl.ds(0, 2 * size)],
+                    a_send.at[dx, zz], r_recv.at[x, zz], to,
+                ).start()
 
         both(is_image, start)
+
+    def start_flat(image):
+        for dx in (1, 3, 2):
+            to = lax.rem(x + dx, XS) * ZS + z
+            for part in range(2):
+                send(
+                    outbound(to, image, part), held.at[:, part, core, landing(me, image, part)],
+                    a_send.at[dx, z], a_recv.at[me], to,
+                ).start()
+
+    both(is_image, start_flat)
 
     @pl.when(jnp.logical_not(is_image))
     def _():
         blank[...] = jnp.zeros_like(blank)
         pltpu.make_async_copy(blank, out_ref.at[pl.ds(TEXT_ROWS, ROWS - TEXT_ROWS)], zero_sem).start()
+
+    def await_rows(image, sem):
+        whole = pay_ref.at[0, :, pl.ds(0, 2 * (IMAGE_HALF if image else TEXT_HALF))]
+        pltpu.make_async_copy(whole, whole, sem).wait()
+
+    @pl.loop(0, ZS - 1)
+    def _(i):
+        zz = far_first(i)
+        for dx in (1, 3, 2):
+            from_x = lax.rem(x + XS - dx, XS)
+
+            def forward(image):
+                size = IMAGE_HALF if image else TEXT_HALF
+                await_rows(image, r_recv.at[from_x, zz])
+                source = from_x * ZS + z
+                for part in range(2):
+                    send(
+                        relay.at[from_x, zz, :, pl.ds(part * size, size)],
+                        held.at[:, part, core, landing(source, image, part)],
+                        r_send.at[from_x, zz], a_recv.at[source], x * ZS + zz,
+                    ).start()
+
+            both(from_x >= XS // 2, forward)
 
     @pl.loop(0, CHIPS)
     def _(i):
@@ -477,13 +530,6 @@
     def _(i):
         to = chip(i)
 
-        def sent(image):
-            size = 2 * (IMAGE_HALF if image else TEXT_HALF)
-            whole = pay_ref.at[0, :, pl.ds(0, size)]
-            pltpu.make_async_copy(whole, whole, a_send.at[to]).wait()
-
-        both(is_image, sent)
-
         def returned(image):
             size = 2 * (IMAGE_HALF if image else TEXT_HALF)
             whole = mixed.at[0, pl.ds(0, size)]
@@ -493,6 +539,27 @@
 
     share(0).wait_send()
     share(1).wait_send()
+
+    def sent(image):
+        @pl.loop(0, ZS)
+        def _(zz):
+            for dx in range(XS):
+
+                @pl.when(jnp.logical_or(zz != z, dx != 0))
+                def _():
+                    await_rows(image, a_send.at[dx, zz])
+
+    both(is_image, sent)
+
+    @pl.loop(1, ZS)
+    def _(i):
+        for dx in range(1, XS):
+            from_x = lax.rem(x + dx, XS)
+
+            def relayed(image):
+                await_rows(image, r_send.at[from_x, lax.rem(z + i, ZS)])
+
+            both(from_x >= XS // 2, relayed)
 
     @pl.when(jnp.logical_not(is_image))
     def _():
@@ -510,11 +577,13 @@
         out_specs=pl.BlockSpec(memory_space=pl.ANY),
         scratch_shapes=[
             pltpu.VMEM((3, 2, 2, PART, HD), jnp.bfloat16),
+            pltpu.VMEM((XS, ZS, 3, 2 * IMAGE_HALF, HD), jnp.bfloat16),
             pltpu.VMEM((2, PART, HD), jnp.float32),
             pltpu.VMEM((2, PART, HD), jnp.float32),
             pltpu.VMEM((2, PART, HD), jnp.bfloat16),
             pltpu.VMEM((ROWS - TEXT_ROWS, WIDTH), jnp.bfloat16),
-            dma((CHIPS,)), dma((CHIPS,)),
+            dma((XS, ZS)), dma((CHIPS,)),
+            dma((XS, ZS)), dma((XS, ZS)),
             dma((2,)), dma((2,)),
             dma((CHIPS,)), dma((CHIPS,)),
             dma,

time: 187 us -> 170 us (0.909)
  Pallas kernels: 167 us -> 150 us
    pallas_call x1, Pallas kernels: 91 us -> 73.7 us  [attend_all(): pl.pallas_call(attend_kernel, name='exchange_attend', out_shape=jax.Shape...]
where the time goes in v2:
time: 170 us; the launch traced here: 169 us
  Pallas kernels  150 us (88%)
  other arithmetic  10.9 us (6%)
  local copies, waits for them, and re-layouts  7.12 us (4%)
    pallas_call x1, Pallas kernels, project(): pl.pallas_call(project_kernel, name='gather_project', out_shape=jax.Shape...  76.4 us
    pallas_call x1, Pallas kernels, attend_all(): pl.pallas_call(attend_kernel, name='exchange_attend', out_shape=jax.Shape...  73.7 us
    reduce_sum x1, other arithmetic, arrival_places(): return jnp.sum(jnp.where(hit, places[:, None, None, :], 0), axis=3)  4.12 us

profile of v2, /device:TPU:1, one launch (start us, length us, event | category | flops | bytes accessed | tf_op | source)
XLA Modules:
  0.0 169.2 jit_solution(8518064008651966237)
XLA Ops:
  0.0 0.7 reduce_window_sum.11
  0.7 0.7 broadcast_add_fusion
  1.4 0.2 dynamic-slice_reduce_fusion
  1.6 0.1 copy.15
  1.7 0.1 le.32
  1.9 0.7 dynamic_slice.9
  2.6 0.9 broadcast_compare_fusion
  3.6 1.3 convert_reduce_fusion
  5.0 4.1 %select_reduce_fusion = s32[2,2,1024]{2,1,0:T(2,128)S(1)} fusion(s32[2,2048]{1,0:T(2,128)S(1)} %get-tuple-element.13, s32[2,1024]{1,0:T(2,128)} %constant.111.clone, s32[2,2048]{1,0:T(2,128)S(1)} %get-tuple-element.14), kind=kLoop, calls=%fused_computation | loop fusion | flops 25161728 | bytes 57344 | tf_op jit(solution)/shard_map/reduce_sum | solution.py:638
  9.1 0.6 broadcast_in_dim.73.kpos_ref
  9.8 0.1 select_reduce_fusion.3
  9.9 1.1 fusion.6
  11.0 0.3 select_reduce_fusion.1
  11.3 0.1 copy.13
  11.4 0.1 reshape.143
  11.5 0.1 copy.14
  11.6 0.1 reshape.144
  11.8 0.1 select_reduce_fusion.2
  11.9 2.5 %fusion = (f32[768,128]{1,0:T(8,128)}, f32[768,128]{1,0:T(8,128)}) fusion(f32[128]{0:T(128)S(1)} %get-tuple-element.11, f32[128]{0:T(128)S(1)} %get-tuple-element.12, f32[768]{0:T(1024)S(1)} %subtract_convert_fusion), kind=kLoop, calls=%fused_computation.5 | loop fusion | flops 196608 | bytes 790528 | tf_op jit(solution)/shard_map/mul | solution.py:656
  14.4 1.4 copy.17.qstart_ref
  15.8 1.3 broadcast_in_dim_squeeze.6.qpos_ref
  17.1 76.4 %gather_project.1.pay_ref = bf16[4,3,768,128]{3,2,1,0:T(8,128)(2,1)} custom-call(bf16[2,3,64,512]{3,2,1,0:T(8,128)(2,1)} %bitcast.10, bf16[768,4096]{1,0:T(8,128)(2,1)} %x_ref.1, f32[2,4096]{1,0:T(2,128)} %gain_ref.1, f32[768,128]{1,0:T(8,128)} %get-tuple-element.10.cos_ref, f32[768,128]{1,0:T(8,128)} %get-tuple-element.9.sin_ref, f32[2,2,512]{2,1,0:T(2,128)} %qk_ref.1), custom_call_target="tpu_custom_call" | custom-call | tf_op jit(solution)/shard_map/gather_project/pallas_call | solution.py:253
  93.5 73.7 %exchange_attend.1 = bf16[768,512]{1,0:T(8,128)(2,1)} custom-call(bf16[4,3,768,128]{3,2,1,0:T(8,128)(2,1)} %gather_project.1.pay_ref, s32[2,2,1,1024]{3,2,1,0:T(1,128)} %broadcast_in_dim.73.kpos_ref, s32[2,1024,1]{2,1,0:T(8,128)} %broadcast_in_dim_squeeze.6.qpos_ref, s32[2,1024,1]{2,1,0:T(8,128)} %copy.17.qstart_ref), custom_call_target="tpu_custom_call" | custom-call | tf_op jit(solution)/shard_map/exchange_attend/pallas_call | solution.py:572
  167.1 2.1 %copy.23 = bf16[768,512]{1,0:T(8,128)(2,1)} copy(bf16[768,512]{1,0:T(8,128)(2,1)} %exchange_attend.1) | data formatting | bytes 1572864
  (18 shorter events, 0.3 us)

commit v3 on v2

--- a/solution.py
+++ b/solution.py
@@ -12,6 +12,7 @@
 BLOCK = 256
 SEQ_LEN = 4096
 SEQS = 8
+DOCS = 4
 BLOCKS = 128
 ROWS = 768
 TEXT_ROWS = 256
@@ -40,9 +41,24 @@
     return lax.div(chip, ZS), lax.rem(chip, ZS), core, lax.axis_index("tp")
 
 
+def start_row(lengths_ref):
+    lane = lax.broadcasted_iota(jnp.int32, (1, 128), 1)
+    row = jnp.full((1, 128), SEQS * SEQ_LEN, jnp.int32)
+    for seq in range(SEQS):
+        start = jnp.int32(seq * SEQ_LEN)
+        for doc in range(DOCS):
+            row = jnp.where(lane == seq * DOCS + doc, start, row)
+            start = start + lengths_ref[seq, doc]
+    return row.astype(jnp.float32)
+
+
+def start_of(token, starts):
+    return jnp.max(jnp.where(starts <= token, starts, 0.0), axis=1, keepdims=True)
+
+
 def project_kernel(
-    w_ref, x_ref, gain_ref, cos_ref, sin_ref, qk_ref, out_ref,
-    weights, rows, normed, acc,
+    lengths_ref, w_ref, x_ref, gain_ref, qk_ref, owner_ref, freq_ref, code_ref, out_ref, places_ref,
+    weights, rows, normed, acc, cos_ref, sin_ref, ranked, turned_owner,
     z_send, z_recv, x_send, x_recv, s_send, s_recv, c_send, c_recv, load_sem, own_sem,
 ):
     x, z, core, tp = place_of()
@@ -128,88 +144,159 @@
                     k = (xx * ZS + zz) * 128
                     normed[zz, pl.ds(at, 16), xx * 128 : xx * 128 + 128] = scaled[:, k : k + 128]
 
+    starts = start_row(lengths_ref)
+    device_id = (2 * (x * ZS + z) + core).astype(jnp.float32)
+
+    def before(shape, axis):
+        down = lax.broadcasted_iota(jnp.int32, shape, 0)
+        right = lax.broadcasted_iota(jnp.int32, shape, 1)
+        return jnp.where(down < right if axis else right < down, 1.0, 0.0).astype(jnp.bfloat16)
+
+    def rank_owned():
+        mine = owner_ref[...].astype(jnp.float32) == device_id
+        marks = jnp.where(mine, 1.0, 0.0).astype(jnp.bfloat16)
+        rank = jnp.dot(marks, before((BLOCK, BLOCK), 1), preferred_element_type=jnp.float32)
+        ranked[...] = jnp.where(mine, rank, 7.0).astype(jnp.bfloat16)
+
+    each = 2 + 4 * modality
+
+    def rope_rows(i):
+        row = lax.broadcasted_iota(jnp.int32, (128, BLOCKS), 0) + i * 128
+        block = lax.broadcasted_iota(jnp.int32, (128, BLOCKS), 1)
+        rank = row - each * block
+        here = (rank >= 0) & (rank < each)
+        wanted = jnp.sum(jnp.where(here, rank, 0).astype(jnp.float32), axis=1, keepdims=True)
+        base = jnp.sum(jnp.where(here, block * BLOCK, 0).astype(jnp.float32), axis=1, keepdims=True)
+        spread = jnp.dot(
+            jnp.where(here, 1.0, 0.0).astype(jnp.bfloat16), ranked[...],
+            preferred_element_type=jnp.float32,
+        )
+        order = lax.broadcasted_iota(jnp.int32, (128, BLOCK), 1).astype(jnp.float32)
+        token = base + jnp.sum(jnp.where(spread == wanted, order, 0.0), axis=1, keepdims=True)
+        angle = (token - start_of(token, starts)) * freq_ref[...]
+        lane = lax.broadcasted_iota(jnp.int32, (128, HD), 1)
+        sine = jnp.sin(angle)
+        cos_ref[pl.ds(i * 128, 128), :] = jnp.cos(angle)
+        sin_ref[pl.ds(i * 128, 128), :] = jnp.where(lane < HD // 2, -sine, sine)
+
+    def turn_owner():
+        down = lax.broadcasted_iota(jnp.int32, (BLOCK, BLOCK), 0)
+        right = lax.broadcasted_iota(jnp.int32, (BLOCK, BLOCK), 1)
+        turned_owner[...] = lax.dot_general(
+            jnp.where(down == right, 1.0, 0.0).astype(jnp.bfloat16),
+            owner_ref[...].astype(jnp.float32).astype(jnp.bfloat16),
+            (((1,), (1,)), ((), ())), preferred_element_type=jnp.float32,
+        ).astype(jnp.bfloat16)
+
+    def arrival_order(part, side):
+        first_block = 16 * lax.div(x * ZS + z, HEADS) + 8 * part
+        block = code_ref[3:4, :] + first_block.astype(jnp.float32)
+        pick = lax.broadcasted_iota(jnp.int32, (BLOCKS, PART), 0).astype(jnp.float32) == block
+        owners = jnp.dot(
+            turned_owner[...], jnp.where(pick, 1.0, 0.0).astype(jnp.bfloat16),
+            preferred_element_type=jnp.float32,
+        )
+        mine = owners == code_ref[side : side + 1, :]
+        rank = jnp.dot(
+            before((BLOCK, BLOCK), 0), jnp.where(mine, 1.0, 0.0).astype(jnp.bfloat16),
+            preferred_element_type=jnp.float32,
+        )
+        order = lax.broadcasted_iota(jnp.int32, (BLOCK, PART), 0).astype(jnp.float32)
+        hit = mine & (rank == code_ref[2:3, :])
+        within = jnp.sum(jnp.where(hit, order, 0.0), axis=0, keepdims=True)
+        places_ref[part, side] = within + block * BLOCK
+
+    def arrive(kind, way, hop):
+        zz = around(-hop if way == 0 else hop)
+
+        def take():
+            along_z(kind, way, hop).wait_recv()
+            if hop < 3:
+                along_z(kind, way, hop + 1).start()
+            if hop == 3:
+
+                @pl.when(long_way(kind) == way)
+                def _():
+                    along_z(kind, way, 4).start()
+
+            if kind == 0:
+                to_partner(zz, zz, x).start()
+            to_sibling(zz, columns[kind]).start()
+
+        if hop == 4:
+            pl.when(long_way(kind) == way)(take)
+        else:
+            take()
+
+    def from_partner(zz):
+        to_partner(zz, zz, x_in).wait_recv()
+        to_sibling(zz, x_in).start()
+
+    def consume(zz, first=False):
+        for xx in range(XS):
+            to_sibling(zz, xx).wait_recv()
+
+        @pl.loop(0, 3)
+        def _(j):
+            part = jnp.dot(
+                normed[zz], weights[zz, j].reshape(XS * 2 * K_CHUNK, WIDTH),
+                preferred_element_type=jnp.float32,
+            )
+            if first:
+                acc[j] = part
+            else:
+                acc[j] += part
+
+    def consume_two(hop):
+        @pl.loop(0, 2)
+        def _(way):
+            consume(around(hop * (2 * way - 1)))
+
     normalize(0)
     normalize(1)
-    put(w_ref.at[modality], spot(z, 3 - x), c_send, c_recv, across).wait_recv()
+    put(mine, spot(z, 3 - x), c_send, c_recv, across).wait_recv()
     to_partner(ZS, z, 3 - x).start()
     for way in range(2):
         along_z(1, way, 1).start()
     to_sibling(z, 3 - x).start()
+    arrive(0, 0, 1)
+    arrive(0, 1, 1)
+    from_partner(z)
     normalize(2)
     normalize(3)
     to_partner(ZS, z, 3 - x_in).wait_recv()
     for way in range(2):
         along_z(2, way, 1).start()
     to_sibling(z, 3 - x_in).start()
-    to_partner(z, z, x_in).wait_recv()
-    to_sibling(z, x_in).start()
     normalize(4)
     normalize(5)
-    own.wait()
-
-    def arrive(kind, way, hop, last):
-        zz = around(-hop if way == 0 else hop)
-        along_z(kind, way, hop).wait_recv()
-        if not last:
-            onward = jnp.logical_or(hop < 3, long_way(kind) == way)
-
-            @pl.when(onward)
-            def _():
-                along_z(kind, way, hop + 1).start()
-
-        if kind == 0:
-            to_partner(zz, zz, x).start()
-        to_sibling(zz, columns[kind]).start()
-
-    def from_partner(zz):
-        to_partner(zz, zz, x_in).wait_recv()
-        to_sibling(zz, x_in).start()
-
-    def consume(zz, first=False):
-        for xx in range(XS):
-            to_sibling(zz, xx).wait_recv()
-        lhs = normed[zz]
-        for j in range(3):
-            part = jnp.dot(
-                lhs, weights[zz, j].reshape(XS * 2 * K_CHUNK, WIDTH),
-                preferred_element_type=jnp.float32,
-            )
-            if first:
-                acc[j] = part
-            else:
-                acc[j] += part
-
-    def hop_step(hop, first):
-        for kind in range(3):
+
+    work = {
+        (1, 1): [rank_owned] + [lambda i=i: rope_rows(i) for i in range(2)],
+        (1, 0): [lambda i=i: rope_rows(i) for i in range(2, 4)],
+        (1, 2): [own.wait, lambda: consume(z, True)],
+        (2, 1): [lambda i=i: rope_rows(i) for i in range(4, 6)],
+        (2, 0): [turn_owner, lambda: arrival_order(0, 0), lambda: arrival_order(0, 1)],
+        (2, 2): [lambda: consume_two(1)],
+        (3, 1): [lambda: arrival_order(1, 0), lambda: arrival_order(1, 1)],
+        (3, 0): [],
+        (3, 2): [lambda: consume_two(2)],
+    }
+    for hop in range(1, 4):
+        for kind in (1, 0, 2):
             for way in range(2):
-                arrive(kind, way, hop, False)
+                arrive(kind, way, hop + 1 if kind == 0 else hop)
+            if kind == 2:
+                for way in range(2):
+                    from_partner(around(-hop if way == 0 else hop))
+            for task in work[hop, kind]:
+                task()
+
+    far = around(4)
+    consume_two(3)
+    for kind in (1, 2):
         for way in range(2):
-            from_partner(around(-hop if way == 0 else hop))
-        if first:
-            consume(z, True)
-
-    hop_step(1, True)
-
-    @pl.loop(2, 4)
-    def _(hop):
-        hop_step(hop, False)
-
-        @pl.loop(0, 2)
-        def _(way):
-            consume(around((hop - 1) * (2 * way - 1)))
-
-    @pl.loop(0, 2)
-    def _(way):
-        consume(around(3 * (2 * way - 1)))
-
-    far = around(4)
-    for kind in range(3):
-        for way in range(2):
-
-            @pl.when(long_way(kind) == way)
-            def _():
-                arrive(kind, way, 4, True)
-
+            arrive(kind, way, 4)
     from_partner(far)
     consume(far)
 
@@ -247,20 +334,28 @@
             to_sibling(zz, xx).wait_send()
 
 
-def project(w, stream, gain, cosines, sines, qk):
+def project(lengths, w, stream, gain, qk, owner, freqs, codes):
     vmem = pl.BlockSpec(memory_space=pltpu.VMEM)
+    smem = pl.BlockSpec(memory_space=pltpu.SMEM)
     dma = pltpu.SemaphoreType.DMA
     return pl.pallas_call(
         project_kernel,
         name="gather_project",
-        out_shape=jax.ShapeDtypeStruct((HEADS, 3, ROWS, HD), jnp.bfloat16),
-        in_specs=[vmem, pl.BlockSpec(memory_space=pl.ANY), vmem, vmem, vmem, vmem],
-        out_specs=vmem,
+        out_shape=(
+            jax.ShapeDtypeStruct((HEADS, 3, ROWS, HD), jnp.bfloat16),
+            jax.ShapeDtypeStruct((2, 2, 1, PART), jnp.float32),
+        ),
+        in_specs=[smem, vmem, pl.BlockSpec(memory_space=pl.ANY), vmem, vmem, vmem, vmem, vmem],
+        out_specs=(vmem, vmem),
         scratch_shapes=[
             pltpu.VMEM((ZS, 3, XS, 2, K_CHUNK, WIDTH), jnp.bfloat16),
             pltpu.VMEM((ROWS, MODEL), jnp.bfloat16),
             pltpu.VMEM((ZS, ROWS, XS * 128), jnp.bfloat16),
             pltpu.VMEM((3, ROWS, WIDTH), jnp.float32),
+            pltpu.VMEM((ROWS, HD), jnp.float32),
+            pltpu.VMEM((ROWS, HD), jnp.float32),
+            pltpu.VMEM((BLOCKS, BLOCK), jnp.bfloat16),
+            pltpu.VMEM((BLOCK, BLOCKS), jnp.bfloat16),
             dma((3, 2, 4)), dma((3, 2, 4)),
             dma((ZS + 1,)), dma((ZS + 1,)),
             dma((ZS, XS)), dma((ZS, XS)),
@@ -270,12 +365,12 @@
         compiler_params=pltpu.CompilerParams(
             collective_id=0, has_side_effects=True, vmem_limit_bytes=60 << 20
         ),
-    )(w, stream, gain, cosines, sines, qk)
+    )(lengths, w, stream, gain, qk, owner, freqs, codes)
 
 
 def attend_kernel(
-    pay_ref, kpos_ref, qpos_ref, qstart_ref, out_ref,
-    held, relay, num, den, mixed, blank,
+    lengths_ref, pay_ref, kpos_ref, out_ref,
+    held, relay, qpos_ref, qstart_ref, num, den, mixed, blank,
     a_send, a_recv, r_send, r_recv, s_send, s_recv, b_send, b_recv, zero_sem,
 ):
     x, z, core, tp = place_of()
@@ -384,6 +479,19 @@
         blank[...] = jnp.zeros_like(blank)
         pltpu.make_async_copy(blank, out_ref.at[pl.ds(TEXT_ROWS, ROWS - TEXT_ROWS)], zero_sem).start()
 
+    starts = start_row(lengths_ref)
+
+    @pl.loop(0, 2)
+    def _(part):
+        down = lax.broadcasted_iota(jnp.int32, (128, 128), 0)
+        right = lax.broadcasted_iota(jnp.int32, (128, 128), 1)
+        row = kpos_ref[part, core]
+        for k in range(PART // 128):
+            at = slice(k * 128, k * 128 + 128)
+            token = jnp.sum(jnp.where(down == right, row[:, at], 0.0), axis=1, keepdims=True)
+            qpos_ref[part, at, :] = token
+            qstart_ref[part, at, :] = start_of(token, starts)
+
     def await_rows(image, sem):
         whole = pay_ref.at[0, :, pl.ds(0, 2 * (IMAGE_HALF if image else TEXT_HALF))]
         pltpu.make_async_copy(whole, whole, sem).wait()
@@ -566,18 +674,20 @@
         pltpu.make_async_copy(blank, out_ref.at[pl.ds(TEXT_ROWS, ROWS - TEXT_ROWS)], zero_sem).wait()
 
 
-def attend_all(payload, key_places, query_places, query_starts):
+def attend_all(lengths, payload, places):
     vmem = pl.BlockSpec(memory_space=pltpu.VMEM)
     dma = pltpu.SemaphoreType.DMA
     return pl.pallas_call(
         attend_kernel,
         name="exchange_attend",
         out_shape=jax.ShapeDtypeStruct((ROWS, WIDTH), jnp.bfloat16),
-        in_specs=[vmem, vmem, vmem, vmem],
+        in_specs=[pl.BlockSpec(memory_space=pltpu.SMEM), vmem, vmem],
         out_specs=pl.BlockSpec(memory_space=pl.ANY),
         scratch_shapes=[
             pltpu.VMEM((3, 2, 2, PART, HD), jnp.bfloat16),
             pltpu.VMEM((XS, ZS, 3, 2 * IMAGE_HALF, HD), jnp.bfloat16),
+            pltpu.VMEM((2, PART, 1), jnp.float32),
+            pltpu.VMEM((2, PART, 1), jnp.float32),
             pltpu.VMEM((2, PART, HD), jnp.float32),
             pltpu.VMEM((2, PART, HD), jnp.float32),
             pltpu.VMEM((2, PART, HD), jnp.bfloat16),
@@ -591,83 +701,29 @@
         compiler_params=pltpu.CompilerParams(
             collective_id=1, has_side_effects=True, vmem_limit_bytes=60 << 20
         ),
-    )(payload, key_places, query_places, query_starts)
-
-
-def doc_starts(doc_lengths):
-    return jnp.cumsum(doc_lengths, axis=1) - doc_lengths
-
-
-def owned_tokens(owner, device, is_image):
-    by_block = owner.reshape(BLOCKS, BLOCK)
-    mask = by_block == device
-    order = np.arange(BLOCK)
-    before = jnp.asarray(order[:, None] < order[None, :], jnp.bfloat16)
-    rank = jnp.dot(mask.astype(jnp.bfloat16), before, preferred_element_type=jnp.float32)
-    tokens = jnp.arange(owner.shape[0], dtype=jnp.int32).reshape(BLOCKS, 1, BLOCK)
-    wanted = jnp.arange(6, dtype=jnp.int32).astype(jnp.float32)[None, :, None]
-    hit = mask[:, None, :] & (rank[:, None, :] == wanted)
-    found = jnp.sum(jnp.where(hit, tokens, 0), axis=2)
-    image = found.reshape(ROWS)
-    text = jnp.pad(found[:, :2].reshape(TEXT_ROWS), (0, ROWS - TEXT_ROWS))
-    return jnp.where(is_image, image, text)
+    )(lengths, payload, places)
 
 
 def arrival_codes():
-    codes = np.zeros((2, PART), np.int32)
-    for core in range(2):
-        at = 0
-        for chip in range(CHIPS):
-            each = 2 if chip < TEXT_CHIPS else 6
-            for block in range(8):
-                for rank in range(each):
-                    codes[core, at] = (block * 64 + 2 * chip + core) * 8 + rank
-                    at += 1
+    codes = np.zeros((8, PART), np.float32)
+    at = 0
+    for chip in range(CHIPS):
+        each = 2 if chip < TEXT_CHIPS else 6
+        for block in range(8):
+            for rank in range(each):
+                codes[:4, at] = (2 * chip, 2 * chip + 1, rank, block)
+                at += 1
     return codes
 
 
-def arrival_places(owner, seq):
-    mine = lax.dynamic_slice_in_dim(owner, seq * SEQ_LEN, SEQ_LEN).reshape(16, BLOCK)
-    order = jnp.arange(BLOCK, dtype=jnp.int32)
-    same = (mine[:, :, None] == mine[:, None, :]) & (order[None, None, :] < order[None, :, None])
-    rank = jnp.sum(same.astype(jnp.int32), axis=2)
-    block = jnp.arange(16, dtype=jnp.int32)[:, None] % 8
-    code = ((block * 64 + mine) * 8 + rank).reshape(2, SEQ_LEN // 2)
-    places = jnp.arange(SEQ_LEN, dtype=jnp.int32).reshape(2, SEQ_LEN // 2)
-    hit = code[:, None, None, :] == jnp.asarray(arrival_codes())[None, :, :, None]
-    return jnp.sum(jnp.where(hit, places[:, None, None, :], 0), axis=3)
-
-
 def on_device(stream, norm_gain, qkv_weight, qk_gain, owner, doc_lengths):
-    device = lax.axis_index("mod")
-    core = device % 2
-    seq = device // 2 // HEADS
-    is_image = device >= 32
-    starts = doc_starts(doc_lengths)
-
-    tokens = owned_tokens(owner, device, is_image)
-    absolute = (starts + jnp.arange(SEQS, dtype=jnp.int32)[:, None] * SEQ_LEN).reshape(-1)
-    first = jnp.max(jnp.where(absolute[None, :] <= tokens[:, None], absolute[None, :], 0), axis=1)
-    half = jnp.arange(HD, dtype=jnp.int32) % (HD // 2)
-    freqs = jnp.exp(-math.log(rope_base) * 2.0 * half.astype(jnp.float32) / HD)
-    angles = (tokens - first).astype(jnp.float32)[:, None] * freqs[None, :]
-    sign = jnp.where(jnp.arange(HD) < HD // 2, -1.0, 1.0).astype(jnp.float32)
-    cosines = jnp.cos(angles)
-    sines = jnp.sin(angles) * sign[None, :]
-
-    key_places = arrival_places(owner, seq)
-    seq_starts = lax.dynamic_slice_in_dim(starts, seq, 1, 0)[0]
-    query_places = lax.dynamic_slice_in_dim(key_places, core, 1, 1)[:, 0]
-    query_starts = jnp.max(
-        jnp.where(seq_starts <= query_places[..., None], seq_starts, 0), axis=-1
+    half = np.arange(HD) % (HD // 2)
+    freqs = np.exp(-math.log(rope_base) * 2.0 * half / HD).astype(np.float32)[None, :]
+    payload, places = project(
+        doc_lengths, jnp.transpose(qkv_weight, (0, 2, 1, 3)), stream, norm_gain, qk_gain,
+        owner.reshape(BLOCKS, BLOCK), jnp.asarray(freqs), jnp.asarray(arrival_codes()),
     )
-
-    payload = project(
-        jnp.transpose(qkv_weight, (0, 2, 1, 3)), stream, norm_gain, cosines, sines, qk_gain
-    )
-    return attend_all(
-        payload, key_places[:, :, None, :], query_places[..., None], query_starts[..., None]
-    )
+    return attend_all(doc_lengths, payload, places)
 
 
 def solution(mesh):

time: 170 us -> 153 us (0.900)
  other arithmetic: 10.9 us -> 0 us
  Pallas kernels: 150 us -> 147 us
  local copies, waits for them, and re-layouts: 7.12 us -> 5.01 us
    reduce_sum x3 -> x0, other arithmetic: 5.71 us -> none  [the longest x1 4.12 us: arrival_places(): return jnp.sum(jnp.where(hit, places[:, None, None, :], 0), axis=3)]
    mul x3 -> x0, other arithmetic: 2.53 us -> none  [the longest x1 2.51 us: on_device(): sines = jnp.sin(angles) * sign[None, :]]
    broadcast_in_dim x2 -> x0, local copies, waits for them, and re-layouts: 1.99 us -> none  [the longest x1 1.38 us: on_device(): query_starts[..., None]]
    unnamed x4 -> x2, local copies, waits for them, and re-layouts: 2.15 us -> 3.41 us
where the time goes in v3:
time: 153 us; the launch traced here: 152 us
  Pallas kernels  147 us (96%)
  local copies, waits for them, and re-layouts  5.01 us (3%)
    pallas_call x1, Pallas kernels, project(): pl.pallas_call(project_kernel, name='gather_project', out_shape=(jax.Shap...  74.9 us
    pallas_call x1, Pallas kernels, attend_all(): pl.pallas_call(attend_kernel, name='exchange_attend', out_shape=jax.Shape...  72.3 us
    unnamed x2, local copies, waits for them, and re-layouts  3.41 us

profile of v3, /device:TPU:1, one launch (start us, length us, event | category | flops | bytes accessed | tf_op | source)
XLA Modules:
  0.0 152.2 jit_solution(10668320129978881506)
XLA Ops:
  0.0 1.3 copy.10.lengths_ref
  1.3 1.6 %reshape.3.owner_ref = s32[128,256]{1,0:T(8,128)} reshape(s32[32768]{0:T(1024)} %param.12) | data formatting | bytes 262144 | tf_op jit(solution)/shard_map/reshape | solution.py:724
  2.9 74.9 %gather_project.1 = (bf16[4,3,768,128]{3,2,1,0:T(8,128)(2,1)}, f32[2,2,1,1024]{3,2,1,0:T(1,128)}) custom-call(s32[8,4]{1,0:T(8,128)} %copy.10.lengths_ref, bf16[2,3,64,512]{3,2,1,0:T(8,128)(2,1)} %bitcast.1, bf16[768,4096]{1,0:T(8,128)(2,1)} %x_ref.1, f32[2,4096]{1,0:T(2,128)} %gain_ref.1, f32[2,2,512]{2,1,0:T(2,128)} %qk_ref.1, ...), custom_call_target="tpu_custom_call" | custom-call | tf_op jit(solution)/shard_map/gather_project/pallas_call | solution.py:341
  77.8 72.3 %exchange_attend.1 = bf16[768,512]{1,0:T(8,128)(2,1)} custom-call(s32[8,4]{1,0:T(8,128)} %copy.10.lengths_ref, bf16[4,3,768,128]{3,2,1,0:T(8,128)(2,1)} %get-tuple-element.7.pay_ref, f32[2,2,1,1024]{3,2,1,0:T(1,128)} %get-tuple-element.8.kpos_ref), custom_call_target="tpu_custom_call" | custom-call | tf_op jit(solution)/shard_map/exchange_attend/pallas_call | solution.py:680
  150.1 2.1 %copy.12 = bf16[768,512]{1,0:T(8,128)(2,1)} copy(bf16[768,512]{1,0:T(8,128)(2,1)} %exchange_attend.1) | data formatting | bytes 1572864

commit v4 on v3

--- a/solution.py
+++ b/solution.py
@@ -29,6 +29,7 @@
 PART = TEXT_CHIPS * (TEXT_HALF + IMAGE_HALF)
 Q_TILE = 256
 MESH = pl.DeviceIdType.MESH
+GROUPS = (pl.ds(0, 2), pl.ds(2, 1))
 
 epsilon = 1e-05
 rope_base = 10000.0
@@ -48,7 +49,7 @@
         start = jnp.int32(seq * SEQ_LEN)
         for doc in range(DOCS):
             row = jnp.where(lane == seq * DOCS + doc, start, row)
-            start = start + lengths_ref[seq, doc]
+            start = start + lengths_ref[doc, seq]
     return row.astype(jnp.float32)
 
 
@@ -58,7 +59,7 @@
 
 def project_kernel(
     lengths_ref, w_ref, x_ref, gain_ref, qk_ref, owner_ref, freq_ref, code_ref, out_ref, places_ref,
-    weights, rows, normed, acc, cos_ref, sin_ref, ranked, turned_owner,
+    weights, rows, normed, acc, cos_ref, sin_ref, blocked, ranked, turned_owner,
     z_send, z_recv, x_send, x_recv, s_send, s_recv, c_send, c_recv, load_sem, own_sem,
 ):
     x, z, core, tp = place_of()
@@ -83,25 +84,38 @@
             device_id=target, device_id_type=MESH,
         )
 
-    def spot(zz, xx):
-        return weights.at[zz, :, xx, core]
-
-    def along_z(kind, way, hop, src=None):
+    def spot(group, zz, xx):
+        return weights.at[zz, GROUPS[group], xx, core]
+
+    def mine(group):
+        return w_ref.at[modality, GROUPS[group]]
+
+    def along_z(group, kind, way, hop, src=None):
         zz = around((1 - hop) if way == 0 else (hop - 1))
-        here = spot(zz, columns[kind])
+        here = spot(group, zz, columns[kind])
+        at = (group, kind, way, hop - 1)
+        return put(
+            here if src is None else src, here, z_send.at[at], z_recv.at[at], z_next[way]
+        )
+
+    def to_partner(group, slot, zz, xx, src=None):
+        here = spot(group, zz, xx)
         return put(
             here if src is None else src, here,
-            z_send.at[kind, way, hop - 1], z_recv.at[kind, way, hop - 1], z_next[way],
-        )
-
-    def to_partner(slot, zz, xx, src=None):
-        here = spot(zz, xx)
-        return put(here if src is None else src, here, x_send.at[slot], x_recv.at[slot], partner)
-
-    def to_sibling(zz, xx, src=None):
-        here = spot(zz, xx)
+            x_send.at[group, slot], x_recv.at[group, slot], partner,
+        )
+
+    def to_sibling(group, zz, xx, src=None):
+        here = spot(group, zz, xx)
         return put(
-            here if src is None else src, here, s_send.at[zz, xx], s_recv.at[zz, xx], sibling
+            here if src is None else src, here,
+            s_send.at[group, zz, xx], s_recv.at[group, zz, xx], sibling,
+        )
+
+    def cross(group):
+        return put(
+            w_ref.at[1 - modality, GROUPS[group]], spot(group, z, x),
+            c_send.at[group], c_recv.at[group], across,
         )
 
     def long_way(kind):
@@ -112,14 +126,13 @@
         pl.semaphore_signal(barrier, inc=1, device_id=target, device_id_type=MESH)
     pl.semaphore_wait(barrier, 5)
 
-    mine = w_ref.at[modality]
-    cross = put(w_ref.at[1 - modality], spot(z, x), c_send, c_recv, across)
-    cross.start()
+    cross(0).start()
     for way in range(2):
-        along_z(0, way, 1, mine).start()
-    to_partner(z, z, x, mine).start()
-    to_sibling(z, x, mine).start()
-    own = pltpu.make_async_copy(mine, spot(z, x), own_sem)
+        along_z(0, 0, way, 1, mine(0)).start()
+    to_partner(0, z, z, x, mine(0)).start()
+    to_sibling(0, z, x, mine(0)).start()
+    cross(1).start()
+    own = pltpu.make_async_copy(w_ref.at[modality], weights.at[z, :, x, core], own_sem)
     own.start()
     pieces = [
         pltpu.make_async_copy(
@@ -152,11 +165,21 @@
         right = lax.broadcasted_iota(jnp.int32, shape, 1)
         return jnp.where(down < right if axis else right < down, 1.0, 0.0).astype(jnp.bfloat16)
 
+    def by_block():
+        row = lax.broadcasted_iota(jnp.int32, (BLOCKS, 2 * BLOCKS), 0)
+        column = lax.broadcasted_iota(jnp.int32, (BLOCKS, 2 * BLOCKS), 1)
+        flat = owner_ref[...].astype(jnp.float32).astype(jnp.bfloat16)
+        for side in range(2):
+            pick = jnp.where(column == 2 * row + side, 1.0, 0.0).astype(jnp.bfloat16)
+            blocked[:, side * 128 : side * 128 + 128] = jnp.dot(
+                pick, flat, preferred_element_type=jnp.float32
+            )
+
     def rank_owned():
-        mine = owner_ref[...].astype(jnp.float32) == device_id
-        marks = jnp.where(mine, 1.0, 0.0).astype(jnp.bfloat16)
+        owned = blocked[...] == device_id
+        marks = jnp.where(owned, 1.0, 0.0).astype(jnp.bfloat16)
         rank = jnp.dot(marks, before((BLOCK, BLOCK), 1), preferred_element_type=jnp.float32)
-        ranked[...] = jnp.where(mine, rank, 7.0).astype(jnp.bfloat16)
+        ranked[...] = jnp.where(owned, rank, 7.0).astype(jnp.bfloat16)
 
     each = 2 + 4 * modality
 
@@ -184,7 +207,7 @@
         right = lax.broadcasted_iota(jnp.int32, (BLOCK, BLOCK), 1)
         turned_owner[...] = lax.dot_general(
             jnp.where(down == right, 1.0, 0.0).astype(jnp.bfloat16),
-            owner_ref[...].astype(jnp.float32).astype(jnp.bfloat16),
+            blocked[...].astype(jnp.bfloat16),
             (((1,), (1,)), ((), ())), preferred_element_type=jnp.float32,
         ).astype(jnp.bfloat16)
 
@@ -196,47 +219,53 @@
             turned_owner[...], jnp.where(pick, 1.0, 0.0).astype(jnp.bfloat16),
             preferred_element_type=jnp.float32,
         )
-        mine = owners == code_ref[side : side + 1, :]
+        same = owners == code_ref[side : side + 1, :]
         rank = jnp.dot(
-            before((BLOCK, BLOCK), 0), jnp.where(mine, 1.0, 0.0).astype(jnp.bfloat16),
+            before((BLOCK, BLOCK), 0), jnp.where(same, 1.0, 0.0).astype(jnp.bfloat16),
             preferred_element_type=jnp.float32,
         )
         order = lax.broadcasted_iota(jnp.int32, (BLOCK, PART), 0).astype(jnp.float32)
-        hit = mine & (rank == code_ref[2:3, :])
+        hit = same & (rank == code_ref[2:3, :])
         within = jnp.sum(jnp.where(hit, order, 0.0), axis=0, keepdims=True)
         places_ref[part, side] = within + block * BLOCK
 
-    def arrive(kind, way, hop):
+    def arrive(group, kind, way, hop):
         zz = around(-hop if way == 0 else hop)
 
         def take():
-            along_z(kind, way, hop).wait_recv()
+            along_z(group, kind, way, hop).wait_recv()
             if hop < 3:
-                along_z(kind, way, hop + 1).start()
+                along_z(group, kind, way, hop + 1).start()
             if hop == 3:
 
                 @pl.when(long_way(kind) == way)
                 def _():
-                    along_z(kind, way, 4).start()
+                    along_z(group, kind, way, 4).start()
 
             if kind == 0:
-                to_partner(zz, zz, x).start()
-            to_sibling(zz, columns[kind]).start()
+                to_partner(group, zz, zz, x).start()
+            to_sibling(group, zz, columns[kind]).start()
 
         if hop == 4:
             pl.when(long_way(kind) == way)(take)
         else:
             take()
 
-    def from_partner(zz):
-        to_partner(zz, zz, x_in).wait_recv()
-        to_sibling(zz, x_in).start()
-
-    def consume(zz, first=False):
+    def from_partner(group, zz):
+        to_partner(group, zz, zz, x_in).wait_recv()
+        to_sibling(group, zz, x_in).start()
+
+    def take_cross(group):
+        put(
+            mine(group), spot(group, z, 3 - x), c_send.at[group], c_recv.at[group], across
+        ).wait_recv()
+        to_partner(group, ZS, z, 3 - x).start()
+
+    def consume(group, zz, first=False):
         for xx in range(XS):
-            to_sibling(zz, xx).wait_recv()
-
-        @pl.loop(0, 3)
+            to_sibling(group, zz, xx).wait_recv()
+
+        @pl.loop(GROUPS[group].start, GROUPS[group].start + GROUPS[group].size)
         def _(j):
             part = jnp.dot(
                 normed[zz], weights[zz, j].reshape(XS * 2 * K_CHUNK, WIDTH),
@@ -247,62 +276,13 @@
             else:
                 acc[j] += part
 
-    def consume_two(hop):
+    def consume_two(group, hop):
         @pl.loop(0, 2)
         def _(way):
-            consume(around(hop * (2 * way - 1)))
-
-    normalize(0)
-    normalize(1)
-    put(mine, spot(z, 3 - x), c_send, c_recv, across).wait_recv()
-    to_partner(ZS, z, 3 - x).start()
-    for way in range(2):
-        along_z(1, way, 1).start()
-    to_sibling(z, 3 - x).start()
-    arrive(0, 0, 1)
-    arrive(0, 1, 1)
-    from_partner(z)
-    normalize(2)
-    normalize(3)
-    to_partner(ZS, z, 3 - x_in).wait_recv()
-    for way in range(2):
-        along_z(2, way, 1).start()
-    to_sibling(z, 3 - x_in).start()
-    normalize(4)
-    normalize(5)
-
-    work = {
-        (1, 1): [rank_owned] + [lambda i=i: rope_rows(i) for i in range(2)],
-        (1, 0): [lambda i=i: rope_rows(i) for i in range(2, 4)],
-        (1, 2): [own.wait, lambda: consume(z, True)],
-        (2, 1): [lambda i=i: rope_rows(i) for i in range(4, 6)],
-        (2, 0): [turn_owner, lambda: arrival_order(0, 0), lambda: arrival_order(0, 1)],
-        (2, 2): [lambda: consume_two(1)],
-        (3, 1): [lambda: arrival_order(1, 0), lambda: arrival_order(1, 1)],
-        (3, 0): [],
-        (3, 2): [lambda: consume_two(2)],
-    }
-    for hop in range(1, 4):
-        for kind in (1, 0, 2):
-            for way in range(2):
-                arrive(kind, way, hop + 1 if kind == 0 else hop)
-            if kind == 2:
-                for way in range(2):
-                    from_partner(around(-hop if way == 0 else hop))
-            for task in work[hop, kind]:
-                task()
-
-    far = around(4)
-    consume_two(3)
-    for kind in (1, 2):
-        for way in range(2):
-            arrive(kind, way, 4)
-    from_partner(far)
-    consume(far)
-
-    @pl.loop(0, ROWS // 128)
-    def _(i):
-        at = pl.ds(pl.multiple_of(i * 128, 128), 128)
+            consume(group, around(hop * (2 * way - 1)))
+
+    def finish_rows(i):
+        at = pl.ds(i * 128, 128)
         cosine = cos_ref[at, :]
         sine = sin_ref[at, :]
         for head in range(HEADS):
@@ -314,24 +294,115 @@
                 scaled = centred * lax.rsqrt(spread + epsilon) * qk_ref[modality, pl.ds(j, 1), lanes]
                 turned = scaled * cosine + pltpu.roll(scaled, HD // 2, 1) * sine
                 out_ref[head, j, at, :] = turned.astype(jnp.bfloat16)
-            out_ref[head, 2, at, :] = acc[2, at, lanes].astype(jnp.bfloat16)
-
-    cross.wait_send()
-    for kind in range(3):
+
+    normalize(0)
+    normalize(1)
+    take_cross(0)
+    for way in range(2):
+        along_z(0, 1, way, 1).start()
+    to_sibling(0, z, 3 - x).start()
+    arrive(0, 0, 0, 1)
+    arrive(0, 0, 1, 1)
+    from_partner(0, z)
+    normalize(2)
+    normalize(3)
+    to_partner(0, ZS, z, 3 - x_in).wait_recv()
+    for way in range(2):
+        along_z(0, 2, way, 1).start()
+    to_sibling(0, z, 3 - x_in).start()
+    normalize(4)
+    normalize(5)
+
+    def start_values():
+        take_cross(1)
+        to_partner(1, z, z, x, mine(1)).start()
+
+    def send_values():
+        to_partner(1, ZS, z, 3 - x_in).wait_recv()
         for way in range(2):
-            for hop in range(1, 4):
-                along_z(kind, way, hop).wait_send()
-
-            @pl.when(long_way(kind) == way)
-            def _():
-                along_z(kind, way, 4).wait_send()
-
-    for slot in range(ZS):
-        to_partner(slot, slot, x).wait_send()
-    to_partner(ZS, z, x).wait_send()
-    for zz in range(ZS):
-        for xx in range(XS):
-            to_sibling(zz, xx).wait_send()
+            along_z(1, 0, way, 1, mine(1)).start()
+        for way in range(2):
+            along_z(1, 1, way, 1).start()
+        for way in range(2):
+            along_z(1, 2, way, 1).start()
+        to_sibling(1, z, x, mine(1)).start()
+        to_sibling(1, z, 3 - x).start()
+        to_sibling(1, z, 3 - x_in).start()
+        from_partner(1, z)
+
+    def hops(group, work):
+        for hop in range(1, 4):
+            for kind in (1, 0, 2):
+                for way in range(2):
+                    arrive(group, kind, way, hop + 1 if kind == 0 else hop)
+                if kind == 2:
+                    for way in range(2):
+                        from_partner(group, around(-hop if way == 0 else hop))
+                for task in work[hop, kind]:
+                    task()
+
+    far = around(4)
+
+    def last_hop(group):
+        for kind in (1, 2):
+            for way in range(2):
+                arrive(group, kind, way, 4)
+        from_partner(group, far)
+
+    hops(0, {
+        (1, 1): [by_block, rank_owned] + [lambda i=i: rope_rows(i) for i in range(2)],
+        (1, 0): [lambda i=i: rope_rows(i) for i in range(2, 4)],
+        (1, 2): [start_values, own.wait, lambda: consume(0, z, True)],
+        (2, 1): [lambda i=i: rope_rows(i) for i in range(4, 6)],
+        (2, 0): [turn_owner, lambda: arrival_order(0, 0), lambda: arrival_order(0, 1)],
+        (2, 2): [send_values, lambda: consume_two(0, 1)],
+        (3, 1): [lambda: arrival_order(1, 0), lambda: arrival_order(1, 1)],
+        (3, 0): [],
+        (3, 2): [lambda: consume_two(0, 2)],
+    })
+    arrive(1, 0, 0, 1)
+    arrive(1, 0, 1, 1)
+    last_hop(0)
+    consume_two(0, 3)
+    finish = [lambda i=i: finish_rows(i) for i in range(ROWS // 128)]
+    hops(1, {
+        (1, 1): [lambda: consume(0, far)],
+        (1, 0): finish[0:1],
+        (1, 2): finish[1:2],
+        (2, 1): finish[2:3],
+        (2, 0): finish[3:4],
+        (2, 2): finish[4:5],
+        (3, 1): finish[5:6],
+        (3, 0): [lambda: consume(1, z, True)],
+        (3, 2): [lambda: consume_two(1, 1), lambda: consume_two(1, 2)],
+    })
+    last_hop(1)
+    consume_two(1, 3)
+    consume(1, far)
+
+    @pl.loop(0, ROWS // 128)
+    def _(i):
+        at = pl.ds(pl.multiple_of(i * 128, 128), 128)
+        for head in range(HEADS):
+            out_ref[head, 2, at, :] = acc[2, at, head * HD : head * HD + HD].astype(jnp.bfloat16)
+
+    for group in range(2):
+        cross(group).wait_send()
+        for kind in range(3):
+            for way in range(2):
+                for hop in range(1, 4):
+                    along_z(group, kind, way, hop).wait_send()
+
+                @pl.when(long_way(kind) == way)
+                def _():
+                    along_z(group, kind, way, 4).wait_send()
+
+        for slot in range(ZS):
+            to_partner(group, slot, slot, x).wait_send()
+        to_partner(group, ZS, z, x).wait_send()
+        for zz in range(ZS):
+            for xx in range(XS):
+                to_sibling(group, zz, xx).wait_send()
 
 
 def project(lengths, w, stream, gain, qk, owner, freqs, codes):
@@ -354,12 +425,13 @@
             pltpu.VMEM((3, ROWS, WIDTH), jnp.float32),
             pltpu.VMEM((ROWS, HD), jnp.float32),
             pltpu.VMEM((ROWS, HD), jnp.float32),
+            pltpu.VMEM((BLOCKS, BLOCK), jnp.float32),
             pltpu.VMEM((BLOCKS, BLOCK), jnp.bfloat16),
             pltpu.VMEM((BLOCK, BLOCKS), jnp.bfloat16),
-            dma((3, 2, 4)), dma((3, 2, 4)),
-            dma((ZS + 1,)), dma((ZS + 1,)),
-            dma((ZS, XS)), dma((ZS, XS)),
-            dma, dma,
+            dma((2, 3, 2, 4)), dma((2, 3, 2, 4)),
+            dma((2, ZS + 1)), dma((2, ZS + 1)),
+            dma((2, ZS, XS)), dma((2, ZS, XS)),
+            dma((2,)), dma((2,)),
             dma((ROWS // 128,)), dma,
         ],
         compiler_params=pltpu.CompilerParams(
@@ -543,107 +615,90 @@
     share(0).start()
     share(1).start()
 
-    def attend(side, first):
-        @pl.loop(0, 2 * PART // Q_TILE)
+    tiles = PART // Q_TILE
+
+    def attend(part, side, first):
+        @pl.loop(0, tiles)
         def _(tile):
-            part = lax.div(tile, PART // Q_TILE)
-            at = pl.ds(
-                pl.multiple_of(lax.rem(tile, PART // Q_TILE) * Q_TILE, Q_TILE), Q_TILE
-            )
+            at = pl.ds(pl.multiple_of(tile * Q_TILE, Q_TILE), Q_TILE)
             query = held[0, part, core, at, :]
             place = qpos_ref[part, at, :]
             start = qstart_ref[part, at, :]
-
-            def step(key_part, fresh):
+            for key_part in range(part + 1):
                 keys = held[1, key_part, side]
                 values = held[2, key_part, side]
                 scores = lax.dot_general(
                     query, keys, (((1,), (1,)), ((), ())), preferred_element_type=jnp.float32
                 )
                 spots = kpos_ref[key_part, side]
-                visible = (spots <= place) & (spots >= start)
+                visible = spots >= start
+                if key_part == part:
+                    visible = visible & (spots <= place)
                 weight = jnp.where(visible, jnp.exp(scores * (1.0 / math.sqrt(HD))), 0.0)
                 total = jnp.sum(weight, axis=1, keepdims=True)
                 product = jnp.dot(
                     weight.astype(jnp.bfloat16), values, preferred_element_type=jnp.float32
                 )
-                if fresh:
+                if first and key_part == 0:
                     num[part, at, :] = product
                     den[part, at, :] = jnp.broadcast_to(total, product.shape)
                 else:
                     num[part, at, :] += product
                     den[part, at, :] += jnp.broadcast_to(total, product.shape)
 
-            step(0, first)
-
-            @pl.when(part == 1)
-            def _():
-                step(1, False)
-
-    attend(core, True)
-    shared(0).wait_recv()
-    shared(1).wait_recv()
-    attend(1 - core, False)
-
-    @pl.loop(0, 2 * PART // Q_TILE)
-    def _(tile):
-        part = lax.div(tile, PART // Q_TILE)
-        at = pl.ds(pl.multiple_of(lax.rem(tile, PART // Q_TILE) * Q_TILE, Q_TILE), Q_TILE)
-        mixed[part, at, :] = (num[part, at, :] / den[part, at, :]).astype(jnp.bfloat16)
-
-    def home(image, part, who_seq, who_head):
+    def finish(part):
+        @pl.loop(0, tiles)
+        def _(tile):
+            at = pl.ds(pl.multiple_of(tile * Q_TILE, Q_TILE), Q_TILE)
+            mixed[part, at, :] = (num[part, at, :] / den[part, at, :]).astype(jnp.bfloat16)
+
+    def home(image, part):
         size = IMAGE_HALF if image else TEXT_HALF
-        at = pl.multiple_of((2 * who_seq + part) * size, 16)
-        return out_ref.at[pl.ds(at, size), pl.ds(pl.multiple_of(who_head * HD, HD), HD)]
-
-    def back(to, image, part):
-        return pltpu.make_async_remote_copy(
-            src_ref=mixed.at[part, landing(to, image, part)],
-            dst_ref=home(image, part, seq, head),
-            send_sem=b_send.at[to], recv_sem=b_recv.at[me],
-            device_id=(2 * to + core, tp), device_id_type=MESH,
-        )
+        at = pl.multiple_of((2 * seq + part) * size, 16)
+        return out_ref.at[pl.ds(at, size), pl.ds(pl.multiple_of(head * HD, HD), HD)]
+
+    def send_home(part):
+        @pl.loop(1, CHIPS)
+        def _(i):
+            to = chip(i)
+
+            def start(image):
+                send(
+                    mixed.at[part, landing(to, image, part)], home(image, part),
+                    b_send.at[part, to], b_recv.at[part, me], to,
+                ).start()
+
+            both(to >= TEXT_CHIPS, start)
+
+        def stay(image):
+            pltpu.make_async_copy(
+                mixed.at[part, landing(me, image, part)], home(image, part), b_recv.at[part, me]
+            ).start()
+
+        both(is_image, stay)
+
+    def await_mixed(image, sem):
+        whole = mixed.at[0, pl.ds(0, IMAGE_HALF if image else TEXT_HALF)]
+        pltpu.make_async_copy(whole, whole, sem).wait()
+
+    for part in range(2):
+        attend(part, core, True)
+        shared(part).wait_recv()
+        attend(part, 1 - core, False)
+        finish(part)
+        send_home(part)
+
+    @pl.loop(0, CHIPS)
+    def _(i):
+        source = chip(-i)
+        for part in range(2):
+            both(is_image, lambda image: await_mixed(image, b_recv.at[part, source]))
 
     @pl.loop(1, CHIPS)
     def _(i):
         to = chip(i)
-
-        def start(image):
-            for part in range(2):
-                back(to, image, part).start()
-
-        both(to >= TEXT_CHIPS, start)
-
-    def back_self(image):
         for part in range(2):
-            pltpu.make_async_copy(
-                mixed.at[part, landing(me, image, part)],
-                home(image, part, seq, head), b_recv.at[me],
-            ).start()
-
-    both(is_image, back_self)
-
-    @pl.loop(0, CHIPS)
-    def _(i):
-        source = chip(-i)
-
-        def arrive(image):
-            size = 2 * (IMAGE_HALF if image else TEXT_HALF)
-            whole = mixed.at[0, pl.ds(0, size)]
-            pltpu.make_async_copy(whole, whole, b_recv.at[source]).wait()
-
-        both(is_image, arrive)
-
-    @pl.loop(1, CHIPS)
-    def _(i):
-        to = chip(i)
-
-        def returned(image):
-            size = 2 * (IMAGE_HALF if image else TEXT_HALF)
-            whole = mixed.at[0, pl.ds(0, size)]
-            pltpu.make_async_copy(whole, whole, b_send.at[to]).wait()
-
-        both(to >= TEXT_CHIPS, returned)
+            both(to >= TEXT_CHIPS, lambda image: await_mixed(image, b_send.at[part, to]))
 
     share(0).wait_send()
     share(1).wait_send()
@@ -695,7 +750,7 @@
             dma((XS, ZS)), dma((CHIPS,)),
             dma((XS, ZS)), dma((XS, ZS)),
             dma((2,)), dma((2,)),
-            dma((CHIPS,)), dma((CHIPS,)),
+            dma((2, CHIPS)), dma((2, CHIPS)),
             dma,
         ],
         compiler_params=pltpu.CompilerParams(
@@ -719,11 +774,12 @@
 def on_device(stream, norm_gain, qkv_weight, qk_gain, owner, doc_lengths):
     half = np.arange(HD) % (HD // 2)
     freqs = np.exp(-math.log(rope_base) * 2.0 * half / HD).astype(np.float32)[None, :]
+    lengths = jnp.transpose(doc_lengths)
     payload, places = project(
-        doc_lengths, jnp.transpose(qkv_weight, (0, 2, 1, 3)), stream, norm_gain, qk_gain,
-        owner.reshape(BLOCKS, BLOCK), jnp.asarray(freqs), jnp.asarray(arrival_codes()),
+        lengths, jnp.transpose(qkv_weight, (0, 2, 1, 3)), stream, norm_gain, qk_gain,
+        owner.reshape(2 * BLOCKS, BLOCK // 2), jnp.asarray(freqs), jnp.asarray(arrival_codes()),
     )
-    return attend_all(doc_lengths, payload, places)
+    return attend_all(lengths, payload, places)
 
 
 def solution(mesh):

time: 153 us -> 139 us (0.908)
  Pallas kernels: 147 us -> 137 us
  local copies, waits for them, and re-layouts: 5.01 us -> 2.06 us
    pallas_call x1, Pallas kernels: 74.9 us -> 69.7 us  [project(): pl.pallas_call(project_kernel, name='gather_project', out_shape=(jax.Shap...]
    pallas_call x1, Pallas kernels: 72.3 us -> 67.3 us  [attend_all(): pl.pallas_call(attend_kernel, name='exchange_attend', out_shape=jax.Shape...]
    reshape x1 -> x0, local copies, waits for them, and re-layouts: 1.6 us -> none  [on_device(): owner.reshape(BLOCKS, BLOCK)]
    unnamed x2 -> x1, local copies, waits for them, and re-layouts: 3.41 us -> 2.06 us
where the time goes in v4:
time: 139 us
  Pallas kernels  137 us (99%)
  local copies, waits for them, and re-layouts  2.06 us (1%)
    pallas_call x1, Pallas kernels, project(): pl.pallas_call(project_kernel, name='gather_project', out_shape=(jax.Shap...  69.7 us
    pallas_call x1, Pallas kernels, attend_all(): pl.pallas_call(attend_kernel, name='exchange_attend', out_shape=jax.Shape...  67.3 us

profile of v4, /device:TPU:1, one launch (start us, length us, event | category | flops | bytes accessed | tf_op | source)
XLA Modules:
  0.0 139.1 jit_solution(5037448535993307437)
XLA Ops:
  0.0 69.7 %gather_project.1 = (bf16[4,3,768,128]{3,2,1,0:T(8,128)(2,1)}, f32[2,2,1,1024]{3,2,1,0:T(1,128)}) custom-call(s32[4,8]{1,0:T(4,128)} %bitcast.5, bf16[2,3,64,512]{3,2,1,0:T(8,128)(2,1)} %bitcast.3, bf16[768,4096]{1,0:T(8,128)(2,1)} %x_ref.1, f32[2,4096]{1,0:T(2,128)} %gain_ref.1, f32[2,2,512]{2,1,0:T(2,128)} %qk_ref.1, s32[256,128]{1,0:T(8,128)} %bitcast.4, ...), custom_call_target="tpu_custom_call" | custom-call | tf_op jit(solution)/shard_map/gather_project/pallas_call | solution.py:412
  69.7 67.3 %exchange_attend.1 = bf16[768,512]{1,0:T(8,128)(2,1)} custom-call(s32[4,8]{1,0:T(4,128)} %bitcast.6, bf16[4,3,768,128]{3,2,1,0:T(8,128)(2,1)} %get-tuple-element.7.pay_ref, f32[2,2,1,1024]{3,2,1,0:T(1,128)} %get-tuple-element.8.kpos_ref), custom_call_target="tpu_custom_call" | custom-call | tf_op jit(solution)/shard_map/exchange_attend/pallas_call | solution.py:735
  137.1 2.1 %copy.10 = bf16[768,512]{1,0:T(8,128)(2,1)} copy(bf16[768,512]{1,0:T(8,128)(2,1)} %exchange_attend.1) | data formatting | bytes 1572864
